TPU v7x, 512 devices: a whole 4x4x16 slice. The times are simulated.
512 devices in a mesh: row: 32 (over x, y, core), col: 16 (over z).
Axes of the slice: x: 4, y: 4, z: 16, core: 2. Of those that a mesh axis runs over, the one named last changes fastest.
Arguments:
- tokens: bfloat16 [256, 8192], P('row', 'col'), may hold values from -6 to 6
- gate_blocks: bfloat16 [16, 32, 10, 128, 128], P('col', 'row'), may hold values from -0.1875 to 0.1875
- up_blocks: bfloat16 [16, 32, 10, 128, 128], P('col', 'row'), may hold values from -0.1875 to 0.1875
- down_blocks: bfloat16 [32, 16, 10, 128, 128], P('row', 'col'), may hold values from -0.09375 to 0.09375
- gate_slots: int32 [16, 32, 10], P('col', 'row'), may hold values from 0 to 32, as said below
- up_slots: int32 [16, 32, 10], P('col', 'row'), may hold values from 0 to 32, as said below
- down_slots: int32 [32, 16, 10], P('row', 'col'), may hold values from 0 to 32, as said below
- out_grad: bfloat16 [256, 8192], P('row', 'col'), may hold values from -6 to 6
Outputs:
- layer_out: bfloat16 [256, 8192], P('row', 'col')
- token_grad: bfloat16 [256, 8192], P('row', 'col')
- gate_grad: float32 [16, 32, 10, 128, 128], P('col', 'row')
- up_grad: float32 [16, 32, 10, 128, 128], P('col', 'row')
- down_grad: float32 [32, 16, 10, 128, 128], P('row', 'col')
Inputs may be any that keep to these rules, and one draw needn't show every extreme that they name: `gate_slots`: in every tile the live slots come first and hold distinct block numbers below 32; the other slots hold 32 and are empty; every tile has a live slot, and some tile has all 10 live. `up_slots`: as for gate_slots. `down_slots`: as for gate_slots, with numbers b naming block row b // 4 and block column b % 4 of a tile.
All inputs are finite; a program needn't handle non-finite values.
Results may differ from a plain program's by a relative error of at most 0.025.
Values may be sent and summed in bfloat16 or wider, within the bound.
No kernel may reach another device: no remote copies, remote signals or barrier semaphores. Data moves between devices by JAX's collectives and lax.ppermute only.
A program may use at most 64 MiB of HBM per device.

v0:
```python
import jax
import jax.numpy as jnp
from jax import lax
from jax.sharding import PartitionSpec as P

FF = 32768


def slot_places(slot_ids, row_blocks, col_blocks):
    is_live = slot_ids < row_blocks * col_blocks
    row_of = jnp.minimum(slot_ids // col_blocks, row_blocks - 1)
    col_of = slot_ids % col_blocks
    return (is_live, row_of, col_of)


def dense_tile(blocks, slot_ids, row_blocks, col_blocks):
    blk_width = blocks.shape[-1]
    is_live, row_of, col_of = slot_places(slot_ids, row_blocks, col_blocks)
    row_hot = (
        (row_of[:, None] == jnp.arange(row_blocks, dtype=jnp.int32)[None, :]) & is_live[:, None]
    ).astype(jnp.bfloat16)
    col_hot = (col_of[:, None] == jnp.arange(col_blocks, dtype=jnp.int32)[None, :]).astype(
        jnp.bfloat16
    )
    placed = jnp.einsum(
        "sr,sc,skn->rkcn", row_hot, col_hot, blocks, preferred_element_type=jnp.float32
    )
    return placed.astype(jnp.bfloat16).reshape(row_blocks * blk_width, col_blocks * blk_width)


def pick_blocks(dense_grad, slot_ids, row_blocks, col_blocks, blk_width):
    is_live, row_of, col_of = slot_places(slot_ids, row_blocks, col_blocks)
    grid = dense_grad.reshape(row_blocks, blk_width, col_blocks, blk_width)
    picked = grid[row_of, :, col_of, :]
    return picked * is_live[:, None, None].astype(jnp.float32)


def times_tile(left_rows, tile):
    return jnp.dot(left_rows, tile, preferred_element_type=jnp.float32)


def times_transposed(right_rows, tile):
    return lax.dot_general(
        right_rows, tile, (((1,), (1,)), ((), ())), preferred_element_type=jnp.float32
    )


def outer_sum(left_rows, right_rows):
    return lax.dot_general(
        left_rows, right_rows, (((0,), (0,)), ((), ())), preferred_element_type=jnp.float32
    )


def activate(gate_val, up_val):
    return (gate_val * jax.nn.sigmoid(gate_val) * up_val).astype(jnp.bfloat16)


def gate_cotangents(hid_grad, gate_val, up_val):
    sig_val = jax.nn.sigmoid(gate_val)
    act_val = gate_val * sig_val
    slope = sig_val * (1.0 + gate_val * (1.0 - sig_val))
    return (
        (hid_grad * up_val * slope).astype(jnp.bfloat16),
        (hid_grad * act_val).astype(jnp.bfloat16),
    )


def per_device(
    tokens, gate_blocks, up_blocks, down_blocks, gate_slots, up_slots, down_slots, out_grad
):
    blk_width = gate_blocks.shape[-1]
    row_devices = lax.axis_size("row")
    dblocks = tokens.shape[1] // blk_width
    fblocks = FF // (blk_width * row_devices)
    gate_ids = gate_slots[0, 0]
    up_ids = up_slots[0, 0]
    down_ids = down_slots[0, 0]
    gate_dense = dense_tile(gate_blocks[0, 0], gate_ids, dblocks, fblocks)
    up_dense = dense_tile(up_blocks[0, 0], up_ids, dblocks, fblocks)
    down_dense = dense_tile(down_blocks[0, 0], down_ids, fblocks, dblocks)
    act_panel, grad_panel = (
        lax.all_gather(tokens, "row", axis=0, tiled=True),
        lax.all_gather(out_grad, "row", axis=0, tiled=True),
    )
    gate_part = times_tile(act_panel, gate_dense)
    up_part = times_tile(act_panel, up_dense)
    gate_val, up_val = (
        lax.psum_scatter(
            gate_part.astype(jnp.bfloat16), "col", scatter_dimension=0, tiled=True
        ).astype(jnp.float32),
        lax.psum_scatter(
            up_part.astype(jnp.bfloat16), "col", scatter_dimension=0, tiled=True
        ).astype(jnp.float32),
    )
    hidden = lax.all_gather(activate(gate_val, up_val), "col", axis=0, tiled=True)
    layer_out = lax.psum_scatter(
        times_tile(hidden, down_dense).astype(jnp.bfloat16), "row", scatter_dimension=0, tiled=True
    )
    down_grad = pick_blocks(outer_sum(hidden, grad_panel), down_ids, fblocks, dblocks, blk_width)
    hid_part = times_transposed(grad_panel, down_dense)
    hid_grad = lax.psum_scatter(
        hid_part.astype(jnp.bfloat16), "col", scatter_dimension=0, tiled=True
    ).astype(jnp.float32)
    gate_share, up_share = gate_cotangents(hid_grad, gate_val, up_val)
    gate_cot, up_cot = (
        lax.all_gather(gate_share, "col", axis=0, tiled=True),
        lax.all_gather(up_share, "col", axis=0, tiled=True),
    )
    gate_grad = pick_blocks(outer_sum(act_panel, gate_cot), gate_ids, dblocks, fblocks, blk_width)
    up_grad = pick_blocks(outer_sum(act_panel, up_cot), up_ids, dblocks, fblocks, blk_width)
    token_grad = lax.psum_scatter(
        (times_transposed(gate_cot, gate_dense) + times_transposed(up_cot, up_dense)).astype(
            jnp.bfloat16
        ),
        "row",
        scatter_dimension=0,
        tiled=True,
    )
    return (
        layer_out,
        token_grad,
        gate_grad[None, None],
        up_grad[None, None],
        down_grad[None, None],
    )


def solution(mesh):
    in_specs = (
        P("row", "col"),
        P("col", "row", None, None, None),
        P("col", "row", None, None, None),
        P("row", "col", None, None, None),
        P("col", "row", None),
        P("col", "row", None),
        P("row", "col", None),
        P("row", "col"),
    )
    out_specs = (
        P("row", "col"),
        P("row", "col"),
        P("col", "row", None, None, None),
        P("col", "row", None, None, None),
        P("row", "col", None, None, None),
    )
    return jax.shard_map(
        per_device, mesh=mesh, in_specs=in_specs, out_specs=out_specs, check_vma=False
    )
```

profile of v0, /device:TPU:1, one launch (start us, length us, event | category | flops | bytes accessed | tf_op | source)
XLA Modules:
  0.0 526.0 jit_solution(12178822904663704871)
XLA Ops:
  7.2 0.0 reduce-scatter.16.cloned.1.call-start
  7.2 0.7 fusion.75
  7.9 0.7 and_select_fusion.11
  8.5 29.2 %all_gather.15 = bf16[256,512]{1,0:T(8,128)(2,1)S(1)} all-gather(bf16[8,512]{1,0:T(8,128)(2,1)} %param.8), channel_id=1, replica_groups=mesh['row'=32,'col'=16] {'row'}, dimensions={0}, use_global_device_ids=true | all-gather | bytes 270336 | tf_op jit(solution)/shard_map/all_gather | solution.py:82
  37.7 1.4 convolution_convert_fusion.2
  39.2 0.5 fusion.1
  39.7 1.0 copy.46
  40.7 0.0 reduce-scatter.16.cloned.1.call-update
  40.7 0.0 reduce-scatter.18.cloned.1.call-start
  40.8 0.4 convolution_convert_fusion.1
  41.3 0.5 fusion.2
  41.8 1.0 copy.48
  42.8 0.0 reduce-scatter.20.cloned.1.call-start
  42.9 1.4 fusion
  44.3 1.7 copy.38
  46.0 24.4 %all_gather.17 = bf16[256,512]{1,0:T(8,128)(2,1)S(1)} all-gather(bf16[8,512]{1,0:T(8,128)(2,1)S(1)} %copy-done.2), channel_id=1, replica_groups=mesh['row'=32,'col'=16] {'row'}, dimensions={0}, use_global_device_ids=true | all-gather | bytes 270336 | tf_op jit(solution)/shard_map/all_gather | solution.py:83
  70.4 0.7 copy-done
  71.1 1.7 fusion.3
  72.9 1.0 copy.50
  73.9 0.0 reduce-scatter.14.cloned.1.call-start
  74.0 25.3 %reduce-scatter.16.cloned.1.call-done = bf16[16,1024]{1,0:T(8,128)(2,1)} async-done(((bf16[256,1024]{1,0:T(8,128)(2,1)}), bf16[16,1024]{1,0:T(8,128)(2,1)}) %reduce-scatter.16.cloned.1.call-update) | async-done | bytes 32784 | tf_op jit(solution)/shard_map/reduce_scatter | solution.py:88
  99.3 71.2 %reduce-scatter.18.cloned.1.call-done = bf16[16,1024]{1,0:T(8,128)(2,1)} async-done(((bf16[256,1024]{1,0:T(8,128)(2,1)}), bf16[16,1024]{1,0:T(8,128)(2,1)}) %reduce-scatter.18.cloned.1.call-update) | async-done | bytes 32784 | tf_op jit(solution)/shard_map/reduce_scatter | solution.py:91
  170.5 70.6 %reduce-scatter.20.cloned.1.call-done = bf16[16,1024]{1,0:T(8,128)(2,1)} async-done(((bf16[256,1024]{1,0:T(8,128)(2,1)}), bf16[16,1024]{1,0:T(8,128)(2,1)}) %reduce-scatter.20.cloned.1.call-update) | async-done | bytes 32784 | tf_op jit(solution)/shard_map/reduce_scatter | solution.py:101
  241.1 0.8 fusion.27
  241.9 24.1 %all_gather.18 = bf16[256,1024]{1,0:T(8,128)(2,1)S(1)} all-gather(bf16[16,1024]{1,0:T(8,128)(2,1)S(1)} %get-tuple-element.6), channel_id=1, replica_groups=mesh['row'=32,'col'=16] {'col'}, dimensions={0}, use_global_device_ids=true | all-gather | bytes 557056 | tf_op jit(solution)/shard_map/all_gather | solution.py:106
  266.0 0.5 fusion.9
  266.5 0.5 convolution_bitcast_fusion.1
  266.9 23.4 %all_gather.19 = bf16[256,1024]{1,0:T(8,128)(2,1)S(1)} all-gather(bf16[16,1024]{1,0:T(8,128)(2,1)S(1)} %get-tuple-element.5), channel_id=1, replica_groups=mesh['row'=32,'col'=16] {'col'}, dimensions={0}, use_global_device_ids=true | all-gather | bytes 557056 | tf_op jit(solution)/shard_map/all_gather | solution.py:107
  290.4 1.8 convolution_bitcast_fusion
  292.2 1.2 fusion.4
  293.3 0.0 reduce-scatter.12.cloned.1.call-start
  293.4 23.6 %all_gather.16 = bf16[256,1024]{1,0:T(8,128)(2,1)S(1)} all-gather(bf16[16,1024]{1,0:T(8,128)(2,1)S(1)} %get-tuple-element.7), channel_id=1, replica_groups=mesh['row'=32,'col'=16] {'col'}, dimensions={0}, use_global_device_ids=true | all-gather | bytes 557056 | tf_op jit(solution)/shard_map/all_gather | solution.py:95
  317.0 2.7 fusion.78
  319.8 2.9 reshape.507
  322.7 3.2 copy.42
  325.9 2.9 reshape.506
  328.8 2.9 copy.41
  331.7 1.7 reshape.505
  333.4 1.9 copy.40
  335.3 2.4 convolution_convert_fusion.6
  337.8 2.2 gather_fusion.2
  340.0 0.9 bitcast_multiply_fusion
  341.0 2.2 gather_fusion.1
  343.2 0.6 gather_fusion
  343.8 0.9 bitcast_multiply_fusion.1
  344.7 0.9 bitcast_multiply_fusion.2
  345.7 69.1 %reduce-scatter.14.cloned.1.call-done = bf16[8,512]{1,0:T(8,128)(2,1)} async-done(((bf16[256,512]{1,0:T(8,128)(2,1)}), bf16[8,512]{1,0:T(8,128)(2,1)}) %reduce-scatter.14.cloned.1.call-update) | async-done | bytes 8208 | tf_op jit(solution)/shard_map/reduce_scatter | solution.py:111
  414.8 104.7 %reduce-scatter.12.cloned.1.call-done = bf16[8,512]{1,0:T(8,128)(2,1)} async-done(((bf16[256,512]{1,0:T(8,128)(2,1)}), bf16[8,512]{1,0:T(8,128)(2,1)}) %reduce-scatter.12.cloned.1.call-update) | async-done | bytes 8208 | tf_op jit(solution)/shard_map/reduce_scatter | solution.py:96
  (28 shorter events, 0.2 us)
Async XLA Ops:
  7.2 92.1 %reduce-scatter.16.cloned.1.call-start = ((), (), s32[]{:S(2)}) async-start(), calls=%async_computation.7 | async-start | bytes 557056 | tf_op jit(solution)/shard_map/reduce_scatter | solution.py:88
  39.1 1.6 copy-start.4
  39.2 1.7 copy-start.1
  40.7 129.8 %reduce-scatter.18.cloned.1.call-start = ((), (), s32[]{:S(2)}) async-start(), calls=%async_computation.8 | async-start | bytes 557056 | tf_op jit(solution)/shard_map/reduce_scatter | solution.py:91
  41.3 1.6 copy-start.5
  42.8 3.2 copy-start.2
  42.8 198.3 %reduce-scatter.20.cloned.1.call-start = ((), (), s32[]{:S(2)}) async-start(), calls=%async_computation.9 | async-start | bytes 557056 | tf_op jit(solution)/shard_map/reduce_scatter | solution.py:101
  46.0 27.9 %copy-start.3 = (s32[1,1,10]{2,1,0:T(1,128)S(1)}, s32[1,1,10]{2,1,0:T(1,128)}, u32[]{:S(2)}) copy-start(s32[1,1,10]{2,1,0:T(1,128)} %param.12) | copy-start | bytes 124
  70.4 0.7 copy-start
  73.9 340.9 %reduce-scatter.14.cloned.1.call-start = ((), (), s32[]{:S(2)}) async-start(), calls=%async_computation.6 | async-start | bytes 270336 | tf_op jit(solution)/shard_map/reduce_scatter | solution.py:111
  293.3 226.1 %reduce-scatter.12.cloned.1.call-start = ((), (), s32[]{:S(2)}) async-start(), calls=%async_computation.5 | async-start | bytes 270336 | tf_op jit(solution)/shard_map/reduce_scatter | solution.py:96
Sparse Core Ops, SparseCore 0:
  40.8 58.4 reduce-scatter.15
  102.6 67.7 reduce-scatter.17
  173.8 67.2 reduce-scatter.19
  293.5 121.2 reduce-scatter.13
  419.5 99.9 reduce-scatter.11
where the time goes:
time: 528 us; the launch traced here: 526 us
  waiting for transfers between devices  341 us (65%)
  blocking collectives  125 us (24%)
  local copies, waits for them, and re-layouts  26 us (5%)
  matrix products  15 us (3%)
  between operations  14 us (3%)
    reduce_scatter x1, waiting for transfers between devices, per_device(): lax.psum_scatter(times_tile(hidden, down_dense).astype(jnp.bfloat16), 'ro...  105 us
    reduce_scatter x1, waiting for transfers between devices, per_device(): lax.psum_scatter(up_part.astype(jnp.bfloat16), 'col', scatter_dimension=0...  71.2 us
    reduce_scatter x1, waiting for transfers between devices, per_device(): lax.psum_scatter(hid_part.astype(jnp.bfloat16), 'col', scatter_dimension=...  70.6 us
    reduce_scatter x1, waiting for transfers between devices, per_device(): lax.psum_scatter((times_transposed(gate_cot, gate_dense) + times_transpos...  69.1 us
    all_gather x1, blocking collectives, per_device(): lax.all_gather(tokens, 'row', axis=0, tiled=True)  29.2 us
    reduce_scatter x1, waiting for transfers between devices, per_device(): lax.psum_scatter(gate_part.astype(jnp.bfloat16), 'col', scatter_dimension...  25.3 us
    all_gather x1, blocking collectives, per_device(): lax.all_gather(out_grad, 'row', axis=0, tiled=True)  24.4 us
    all_gather x1, blocking collectives, per_device(): lax.all_gather(gate_share, 'col', axis=0, tiled=True)  24.1 us
  transfers between devices with their start and end apart: 5, of which 5 were waited for; matrix products, arithmetic and copies ran while one was open for 7% of the time, Pallas kernels for 0%

commit v1 on v0

v1 whole, which is shorter than its diff:
```python
import jax
import jax.numpy as jnp
from jax import lax
from jax.experimental import pallas as pl
from jax.experimental.pallas import tpu as pltpu
from jax.sharding import PartitionSpec as P

BLK = 128
F32 = jnp.float32
BF16 = jnp.bfloat16
VMEM_BYTES = 20 * 2**20


def call(kernel, scalars, arrays, outs, scratch=(), name=None):
    in_specs = [pl.BlockSpec(memory_space=pltpu.SMEM) for _ in scalars]
    in_specs += [pl.BlockSpec(memory_space=pltpu.VMEM) for _ in arrays]
    return pl.pallas_call(
        kernel,
        out_shape=[jax.ShapeDtypeStruct(shape, dtype) for shape, dtype in outs],
        in_specs=in_specs,
        out_specs=[pl.BlockSpec(memory_space=pltpu.VMEM) for _ in outs],
        scratch_shapes=list(scratch),
        compiler_params=pltpu.CompilerParams(vmem_limit_bytes=VMEM_BYTES),
        name=name,
    )(*scalars, *arrays)


def at(index, size):
    return pl.ds(pl.multiple_of(index * size, size), size)


def dot(left, right, left_dim, right_dim):
    return lax.dot_general(
        left, right, (((left_dim,), (right_dim,)), ((), ())), preferred_element_type=F32
    )


def place_kernel(slots, gate_blk, up_blk, down_blk, gate_ref, up_ref, down_ref):
    tiles = ((gate_blk, gate_ref), (up_blk, up_ref), (down_blk, down_ref))
    for which, (blk, ref) in enumerate(tiles):
        ref[...] = jnp.zeros_like(ref)
        col_blocks = ref.shape[1] // BLK
        total = (ref.shape[0] // BLK) * col_blocks
        for slot in range(blk.shape[0]):
            number = slots[which, slot]

            @pl.when(number < total)
            def _(number=number, slot=slot, blk=blk, ref=ref, col_blocks=col_blocks):
                ref[at(number // col_blocks, BLK), at(number % col_blocks, BLK)] = blk[slot]


def partial_kernel(place, panel, gate_w, up_w, down_w, p0, p1, p2a, p2b, p3, xs):
    rows = panel.shape[0] // 4
    width = gate_w.shape[0]
    hid = gate_w.shape[1]
    half = p2a.shape[1]
    for off in range(4):
        cls = lax.rem(place[0] + off, 4)
        xs[off * rows : (off + 1) * rows, :] = panel[at(cls, rows), :]
    act, grad = xs[:, :width], xs[:, width:]
    terms = (
        dot(act, gate_w[...], 1, 0),
        dot(act, up_w[...], 1, 0),
        dot(grad, down_w[...], 1, 1),
    )
    for which, term in enumerate(terms):
        term = term.astype(BF16)
        lo = which * hid
        p0[:, lo : lo + hid] = term[:rows]
        p1[:, lo : lo + hid] = term[rows : 2 * rows]
        p3[:, lo : lo + hid] = term[3 * rows :]
        mid = term[2 * rows : 3 * rows]
        in_a = min(max(half - lo, 0), hid)
        if in_a > 0:
            p2a[:, lo : lo + in_a] = mid[:, :in_a]
        if in_a < hid:
            p2b[:, lo + in_a - half : lo + hid - half] = mid[:, in_a:]


def near_sum_kernel(place, p0, r1, r3, ra, rb, s0, s1, s2, s3):
    rows = p0.shape[0] // 4
    half = ra.shape[1]
    for off, out in enumerate((s0, s1, s2, s3)):
        part = at(lax.rem(place[1] + off, 4), rows)
        near = p0[part, :].astype(F32) + r1[part, :].astype(F32) + r3[part, :].astype(F32)
        out[:, :half] = (near[:, :half] + ra[part, :].astype(F32)).astype(out.dtype)
        out[:, half:] = (near[:, half:] + rb[part, :].astype(F32)).astype(out.dtype)


def hidden_kernel(s0, t1, t2, t3, out):
    hid = out.shape[1] // 3

    def total(which):
        cols = slice(which * hid, (which + 1) * hid)
        return (
            s0[:, cols]
            + t1[:, cols].astype(F32)
            + t2[:, cols].astype(F32)
            + t3[:, cols].astype(F32)
        )

    gate, up, cot = total(0), total(1), total(2)
    sig = jax.nn.sigmoid(gate)
    act = gate * sig
    out[:, :hid] = (act * up).astype(BF16)
    out[:, hid : 2 * hid] = (cot * up * (sig * (1.0 + gate * (1.0 - sig)))).astype(BF16)
    out[:, 2 * hid :] = (cot * act).astype(BF16)


def quad_kernel(place, own, v1, v2, v3, whole, low, high):
    rows = own.shape[0]
    half = low.shape[1]
    for off, ref in enumerate((own, v3, v2, v1)):
        part = at(lax.rem(place[1] + off, 4), rows)
        whole[part, :] = ref[...]
        low[part, :] = ref[:, :half]
        high[part, :] = ref[:, half:]


def output_kernel(place, own, w1, wa, wb, w3, gate_w, up_w, down_w, panel, out):
    rows = own.shape[0]
    half = wa.shape[1]
    hid = gate_w.shape[1]
    width = gate_w.shape[0]
    for off, ref in ((0, own), (1, w3), (3, w1)):
        panel[at(lax.rem(place[0] + off, 4), rows), :] = ref[...]
    part = at(lax.rem(place[0] + 2, 4), rows)
    panel[part, :half] = wa[...]
    panel[part, half:] = wb[...]
    out[:, :width] = dot(panel[:, :hid], down_w[...], 1, 0).astype(BF16)
    out[:, width:] = (
        dot(panel[:, hid : 2 * hid], gate_w[...], 1, 1)
        + dot(panel[:, 2 * hid :], up_w[...], 1, 1)
    ).astype(BF16)


def grad_kernel(slots, panel, hidden, gate_out, up_out, down_out, act_t, hid_t):
    width = panel.shape[1] // 2
    hid = hidden.shape[1] // 3
    for blk in range(width // BLK):
        act_t[blk] = panel[:, blk * BLK : (blk + 1) * BLK].T
    for blk in range(hid // BLK):
        hid_t[blk] = hidden[:, blk * BLK : (blk + 1) * BLK].T
    jobs = (
        (act_t, hidden, hid, hid // BLK, gate_out),
        (act_t, hidden, 2 * hid, hid // BLK, up_out),
        (hid_t, panel, width, width // BLK, down_out),
    )
    for which, (left, right, base, col_blocks, out) in enumerate(jobs):
        total = left.shape[0] * col_blocks
        for slot in range(out.shape[0]):
            number = slots[which, slot]
            live = number < total

            @pl.when(live)
            def _(number=number, slot=slot, left=left, right=right, base=base, out=out, n=col_blocks):
                cols = at(base // BLK + number % n, BLK)
                out[slot] = dot(left[number // n], right[:, cols], 1, 0)

            @pl.when(jnp.logical_not(live))
            def _(slot=slot, out=out):
                out[slot] = jnp.zeros(out.shape[1:], F32)


def sum_kernel(parts, out):
    out[...] = jnp.sum(parts[...].astype(F32), axis=0).astype(BF16)


def per_device(
    tokens, gate_blocks, up_blocks, down_blocks, gate_slots, up_slots, down_slots, out_grad
):
    n_row, n_col = lax.axis_size("row"), lax.axis_size("col")
    local, width = tokens.shape
    count = local * n_row
    share = count // n_col
    rows = share * (n_col // 4)
    hid = 8 * BLK
    wide = 3 * hid
    half = wide // 2
    z = lax.axis_index("col")
    place = jnp.stack([z % 4, z // 4]).astype(jnp.int32)
    slots = jnp.stack([gate_slots[0, 0], up_slots[0, 0], down_slots[0, 0]])

    def shift(value, dist):
        return lax.ppermute(value, "col", [(i, (i + dist) % n_col) for i in range(n_col)])

    gate_w, up_w, down_w = call(
        place_kernel,
        (slots,),
        (gate_blocks[0, 0], up_blocks[0, 0], down_blocks[0, 0]),
        (((width, hid), BF16), ((width, hid), BF16), ((hid, width), BF16)),
        name="place",
    )
    both = jnp.concatenate([tokens, out_grad], axis=1)
    spread = jnp.broadcast_to(both[None], (n_row, local, 2 * width))
    panel = lax.all_to_all(spread, "row", 0, 0, tiled=True).reshape(count, 2 * width)

    p0, p1, p2a, p2b, p3 = call(
        partial_kernel,
        (place,),
        (panel, gate_w, up_w, down_w),
        (
            ((rows, wide), BF16),
            ((rows, wide), BF16),
            ((rows, half), BF16),
            ((rows, half), BF16),
            ((rows, wide), BF16),
        ),
        (pltpu.VMEM((count, 2 * width), BF16),),
        name="partials",
    )
    r1, r3, ra, rb = shift(p1, 1), shift(p3, -1), shift(p2a, -2), shift(p2b, 2)
    s0, s1, s2, s3 = call(
        near_sum_kernel,
        (place,),
        (p0, r1, r3, ra, rb),
        (((share, wide), F32),) + (((share, wide), BF16),) * 3,
        name="near_sum",
    )
    t1, t3, t2 = shift(s1, 4), shift(s3, -4), shift(s2, 8)
    (own,) = call(hidden_kernel, (), (s0, t1, t2, t3), (((share, wide), BF16),), name="hidden")

    v1, v3, v2 = shift(own, 4), shift(own, -4), shift(own, 8)
    whole, low, high = call(
        quad_kernel,
        (place,),
        (own, v1, v2, v3),
        (((rows, wide), BF16), ((rows, half), BF16), ((rows, half), BF16)),
        name="quad",
    )
    w1, w3, wa, wb = shift(whole, 1), shift(whole, -1), shift(low, 2), shift(high, -2)
    hidden, out_terms = call(
        output_kernel,
        (place,),
        (whole, w1, wa, wb, w3, gate_w, up_w, down_w),
        (((count, wide), BF16), ((count, 2 * width), BF16)),
        name="outputs",
    )
    parts = lax.all_to_all(
        out_terms.reshape(n_row, local, 2 * width), "row", 0, 0, tiled=True
    )
    gate_grad, up_grad, down_grad = call(
        grad_kernel,
        (slots,),
        (panel, hidden),
        tuple((ref.shape[2:], F32) for ref in (gate_blocks, up_blocks, down_blocks)),
        (
            pltpu.VMEM((width // BLK, BLK, count), BF16),
            pltpu.VMEM((hid // BLK, BLK, count), BF16),
        ),
        name="grads",
    )
    (summed,) = call(sum_kernel, (), (parts,), (((local, 2 * width), BF16),), name="row_sum")
    return (
        summed[:, :width],
        summed[:, width:],
        gate_grad[None, None],
        up_grad[None, None],
        down_grad[None, None],
    )


def solution(mesh):
    in_specs = (
        P("row", "col"),
        P("col", "row", None, None, None),
        P("col", "row", None, None, None),
        P("row", "col", None, None, None),
        P("col", "row", None),
        P("col", "row", None),
        P("row", "col", None),
        P("row", "col"),
    )
    out_specs = (
        P("row", "col"),
        P("row", "col"),
        P("col", "row", None, None, None),
        P("col", "row", None, None, None),
        P("row", "col", None, None, None),
    )
    return jax.shard_map(
        per_device, mesh=mesh, in_specs=in_specs, out_specs=out_specs, check_vma=False
    )
```

time: 528 us -> 164 us (0.31)
  waiting for transfers between devices: 341 us -> 59.9 us
  blocking collectives: 125 us -> 0 us
  starting transfers between devices: 0.21 us -> 83.1 us
  local copies, waits for them, and re-layouts: 26 us -> 7.23 us
  matrix products: 15 us -> 0 us
  between operations: 14 us -> 0.97 us
  Pallas kernels: 0 us -> 10.8 us
    reduce_scatter x5 -> x0, waiting for transfers between devices: 341 us -> none  [the longest x1 105 us: per_device(): lax.psum_scatter(times_tile(hidden, down_dense).astype(jnp.bfloat16), 'ro...]
    all_gather x5 -> x0, blocking collectives: 125 us -> none  [the longest x1 29.2 us: per_device(): lax.all_gather(tokens, 'row', axis=0, tiled=True)]
    ppermute x0 -> x14, starting transfers between devices: none -> 67.8 us  [shift(): lax.ppermute(value, 'col', [(i, (i + dist) % n_col) for i in range(n_col)])]
    ppermute x0 -> x14, waiting for transfers between devices: none -> 45.4 us  [shift(): lax.ppermute(value, 'col', [(i, (i + dist) % n_col) for i in range(n_col)])]
    reshape x6 -> x0, local copies, waits for them, and re-layouts: 15.6 us -> none  [pick_blocks(): grid = dense_grad.reshape(row_blocks, blk_width, col_blocks, blk_width)]
    all_to_all x0 -> x2, starting transfers between devices: none -> 15.3 us  [the longest x1 10.4 us: per_device(): lax.all_to_all(spread, 'row', 0, 0, tiled=True).reshape(count, 2 * width)]
    dot_general x12 -> x0, matrix products: 15 us -> none  [the longest x3 4.99 us: outer_sum(): lax.dot_general(left_rows, right_rows, (((0,), (0,)), ((), ())), preferre...]
    all_to_all x0 -> x2, waiting for transfers between devices: none -> 14.5 us  [the longest x1 8.46 us: per_device(): lax.all_to_all(spread, 'row', 0, 0, tiled=True).reshape(count, 2 * width)]
  transfers between devices with their start and end apart: 5 -> 16, of which waited for: 5 -> 9; matrix products, arithmetic and copies ran while one was open for 7% -> 0% of each run, Pallas kernels for 0% -> 3%
where the time goes in v1:
time: 164 us; the launch traced here: 163 us
  starting transfers between devices  83.1 us (51%)
  waiting for transfers between devices  59.9 us (37%)
  Pallas kernels  10.8 us (7%)
  local copies, waits for them, and re-layouts  7.23 us (4%)
    ppermute x14, starting transfers between devices, shift(): lax.ppermute(value, 'col', [(i, (i + dist) % n_col) for i in range(n_col)])  67.8 us
    ppermute x14, waiting for transfers between devices, shift(): lax.ppermute(value, 'col', [(i, (i + dist) % n_col) for i in range(n_col)])  45.4 us
    pallas_call x8, Pallas kernels, call(): pl.pallas_call(kernel, out_shape=[jax.ShapeDtypeStruct(shape, dtype) for...  10.8 us
    all_to_all x1, starting transfers between devices, per_device(): lax.all_to_all(spread, 'row', 0, 0, tiled=True).reshape(count, 2 * width)  10.4 us
    all_to_all x1, waiting for transfers between devices, per_device(): lax.all_to_all(spread, 'row', 0, 0, tiled=True).reshape(count, 2 * width)  8.46 us
    all_to_all x1, waiting for transfers between devices, per_device(): lax.all_to_all(out_terms.reshape(n_row, local, 2 * width), 'row', 0, 0, t...  6.04 us
    unnamed x22, local copies, waits for them, and re-layouts  5.77 us
    all_to_all x1, starting transfers between devices, per_device(): lax.all_to_all(out_terms.reshape(n_row, local, 2 * width), 'row', 0, 0, t...  4.89 us
  transfers between devices with their start and end apart: 16, of which 9 were waited for; matrix products, arithmetic and copies ran while one was open for 0% of the time, Pallas kernels for 3%

profile of v1, /device:TPU:1, one launch (start us, length us, event | category | flops | bytes accessed | tf_op | source)
XLA Modules:
  0.0 162.8 jit_solution(3747090580482570741)
XLA Ops:
  0.7 0.8 pad_maximum_fusion
  1.5 0.9 broadcast_in_dim.15
  2.3 10.4 %all-to-all-start = ((bf16[32,8,1024]{2,1,0:T(8,128)(2,1)}), bf16[32,8,1024]{2,1,0:T(8,128)(2,1)S(1)}, u32[]{:S(2)}, u32[]{:S(2)}) async-start(bf16[32,8,1024]{2,1,0:T(8,128)(2,1)} %broadcast_in_dim.15), calls=%async_computation | async-start | bytes 1048576 | tf_op jit(solution)/shard_map/all_to_all | solution.py:196
  12.8 0.0 copy-start.7
  12.8 1.0 copy-done.7
  13.8 1.1 place.1
  14.9 1.0 copy-done
  15.9 0.1 pad_add_fusion.1.place
  16.0 8.5 %all-to-all-done = bf16[32,8,1024]{2,1,0:T(8,128)(2,1)S(1)} async-done(((bf16[32,8,1024]{2,1,0:T(8,128)(2,1)}), bf16[32,8,1024]{2,1,0:T(8,128)(2,1)S(1)}, u32[]{:S(2)}, u32[]{:S(2)}) %all-to-all-start) | async-done | bytes 524320 | tf_op jit(solution)/shard_map/all_to_all | solution.py:196
  24.4 1.2 copy-done.1
  25.6 1.5 partials.1
  27.2 2.1 %collective-permute-start = (bf16[64,3072]{1,0:T(8,128)(2,1)S(1)}, bf16[64,3072]{1,0:T(8,128)(2,1)S(1)}, u32[]{:S(2)}, u32[]{:S(2)}) collective-permute-start(bf16[64,3072]{1,0:T(8,128)(2,1)S(1)} %get-tuple-element.29), channel_id=1, source_target_pairs={{0,1},{1,2},{2,3},{3,4},{4,5},{5,6},{6,7},{7,8},{8,9},{9,10},{10,1... | collective-permute-start | bytes 1179656 | tf_op jit(solution)/shard_map/ppermute | solution.py:185
  29.2 9.2 %collective-permute-start.1 = (bf16[64,3072]{1,0:T(8,128)(2,1)S(1)}, bf16[64,3072]{1,0:T(8,128)(2,1)S(1)}, u32[]{:S(2)}, u32[]{:S(2)}) collective-permute-start(bf16[64,3072]{1,0:T(8,128)(2,1)S(1)} %get-tuple-element.30), channel_id=1, source_target_pairs={{0,15},{1,0},{2,1},{3,2},{4,3},{5,4},{6,5},{7,6},{8,7},{9,8},{10,9... | collective-permute-start | bytes 1179656 | tf_op jit(solution)/shard_map/ppermute | solution.py:185
  38.5 3.8 %collective-permute-start.2 = (bf16[64,1536]{1,0:T(8,128)(2,1)S(1)}, bf16[64,1536]{1,0:T(8,128)(2,1)S(1)}, u32[]{:S(2)}, u32[]{:S(2)}) collective-permute-start(bf16[64,1536]{1,0:T(8,128)(2,1)S(1)} %get-tuple-element.31), channel_id=1, source_target_pairs={{0,14},{1,15},{2,0},{3,1},{4,2},{5,3},{6,4},{7,5},{8,6},{9,7},{10,... | collective-permute-start | bytes 589832 | tf_op jit(solution)/shard_map/ppermute | solution.py:185
  42.3 2.4 %collective-permute-start.3 = (bf16[64,1536]{1,0:T(8,128)(2,1)S(1)}, bf16[64,1536]{1,0:T(8,128)(2,1)S(1)}, u32[]{:S(2)}, u32[]{:S(2)}) collective-permute-start(bf16[64,1536]{1,0:T(8,128)(2,1)S(1)} %get-tuple-element.32), channel_id=1, source_target_pairs={{0,2},{1,3},{2,4},{3,5},{4,6},{5,7},{6,8},{7,9},{8,10},{9,11},{10,... | collective-permute-start | bytes 589832 | tf_op jit(solution)/shard_map/ppermute | solution.py:185
  44.7 11.0 %collective-permute-done.2.ra = bf16[64,1536]{1,0:T(8,128)(2,1)S(1)} collective-permute-done((bf16[64,1536]{1,0:T(8,128)(2,1)S(1)}, bf16[64,1536]{1,0:T(8,128)(2,1)S(1)}, u32[]{:S(2)}, u32[]{:S(2)}) %collective-permute-start.2) | collective-permute-done | bytes 196640 | tf_op jit(solution)/shard_map/ppermute | solution.py:185
  55.6 1.0 collective-permute-done.3.rb
  56.7 0.0 collective-permute-done.r1
  56.7 0.0 collective-permute-done.1.r3
  56.7 0.7 near_sum.1
  57.4 3.9 %collective-permute-start.4 = (bf16[16,3072]{1,0:T(8,128)(2,1)S(1)}, bf16[16,3072]{1,0:T(8,128)(2,1)S(1)}, u32[]{:S(2)}, u32[]{:S(2)}) collective-permute-start(bf16[16,3072]{1,0:T(8,128)(2,1)S(1)} %get-tuple-element.34), channel_id=1, source_target_pairs={{0,4},{1,5},{2,6},{3,7},{4,8},{5,9},{6,10},{7,11},{8,12},{9,13},{1... | collective-permute-start | bytes 294920 | tf_op jit(solution)/shard_map/ppermute | solution.py:185
  61.3 8.4 %collective-permute-start.5 = (bf16[16,3072]{1,0:T(8,128)(2,1)S(1)}, bf16[16,3072]{1,0:T(8,128)(2,1)S(1)}, u32[]{:S(2)}, u32[]{:S(2)}) collective-permute-start(bf16[16,3072]{1,0:T(8,128)(2,1)S(1)} %get-tuple-element.35), channel_id=1, source_target_pairs={{0,8},{1,9},{2,10},{3,11},{4,12},{5,13},{6,14},{7,15},{8,0},{9,1},... | collective-permute-start | bytes 294920 | tf_op jit(solution)/shard_map/ppermute | solution.py:185
  69.7 5.2 %collective-permute-start.6 = (bf16[16,3072]{1,0:T(8,128)(2,1)S(1)}, bf16[16,3072]{1,0:T(8,128)(2,1)S(1)}, u32[]{:S(2)}, u32[]{:S(2)}) collective-permute-start(bf16[16,3072]{1,0:T(8,128)(2,1)S(1)} %get-tuple-element.36), channel_id=1, source_target_pairs={{0,12},{1,13},{2,14},{3,15},{4,0},{5,1},{6,2},{7,3},{8,4},{9,5},{1... | collective-permute-start | bytes 294920 | tf_op jit(solution)/shard_map/ppermute | solution.py:185
  74.9 0.0 collective-permute-done.4.t1
  74.9 6.8 %collective-permute-done.5.t2 = bf16[16,3072]{1,0:T(8,128)(2,1)S(1)} collective-permute-done((bf16[16,3072]{1,0:T(8,128)(2,1)S(1)}, bf16[16,3072]{1,0:T(8,128)(2,1)S(1)}, u32[]{:S(2)}, u32[]{:S(2)}) %collective-permute-start.5) | collective-permute-done | bytes 98336 | tf_op jit(solution)/shard_map/ppermute | solution.py:185
  81.8 6.9 %collective-permute-done.6.t3 = bf16[16,3072]{1,0:T(8,128)(2,1)S(1)} collective-permute-done((bf16[16,3072]{1,0:T(8,128)(2,1)S(1)}, bf16[16,3072]{1,0:T(8,128)(2,1)S(1)}, u32[]{:S(2)}, u32[]{:S(2)}) %collective-permute-start.6) | collective-permute-done | bytes 98336 | tf_op jit(solution)/shard_map/ppermute | solution.py:185
  88.7 0.1 hidden.1.own
  88.8 5.4 %collective-permute-start.9 = (bf16[16,3072]{1,0:T(8,128)(2,1)S(1)}, bf16[16,3072]{1,0:T(8,128)(2,1)S(1)}, u32[]{:S(2)}, u32[]{:S(2)}) collective-permute-start(bf16[16,3072]{1,0:T(8,128)(2,1)S(1)} %hidden.1.own), channel_id=1, source_target_pairs={{0,12},{1,13},{2,14},{3,15},{4,0},{5,1},{6,2},{7,3},{8,4},{9,5},{1... | collective-permute-start | bytes 294920 | tf_op jit(solution)/shard_map/ppermute | solution.py:185
  94.2 5.8 %collective-permute-start.8 = (bf16[16,3072]{1,0:T(8,128)(2,1)S(1)}, bf16[16,3072]{1,0:T(8,128)(2,1)S(1)}, u32[]{:S(2)}, u32[]{:S(2)}) collective-permute-start(bf16[16,3072]{1,0:T(8,128)(2,1)S(1)} %hidden.1.own), channel_id=1, source_target_pairs={{0,8},{1,9},{2,10},{3,11},{4,12},{5,13},{6,14},{7,15},{8,0},{9,1},... | collective-permute-start | bytes 294920 | tf_op jit(solution)/shard_map/ppermute | solution.py:185
  100.0 5.8 %collective-permute-start.7 = (bf16[16,3072]{1,0:T(8,128)(2,1)S(1)}, bf16[16,3072]{1,0:T(8,128)(2,1)S(1)}, u32[]{:S(2)}, u32[]{:S(2)}) collective-permute-start(bf16[16,3072]{1,0:T(8,128)(2,1)S(1)} %hidden.1.own), channel_id=1, source_target_pairs={{0,4},{1,5},{2,6},{3,7},{4,8},{5,9},{6,10},{7,11},{8,12},{9,13},{1... | collective-permute-start | bytes 294920 | tf_op jit(solution)/shard_map/ppermute | solution.py:185
  105.8 4.5 %collective-permute-done.8.v2 = bf16[16,3072]{1,0:T(8,128)(2,1)S(1)} collective-permute-done((bf16[16,3072]{1,0:T(8,128)(2,1)S(1)}, bf16[16,3072]{1,0:T(8,128)(2,1)S(1)}, u32[]{:S(2)}, u32[]{:S(2)}) %collective-permute-start.8) | collective-permute-done | bytes 98336 | tf_op jit(solution)/shard_map/ppermute | solution.py:185
  110.4 4.2 %collective-permute-done.7.v1 = bf16[16,3072]{1,0:T(8,128)(2,1)S(1)} collective-permute-done((bf16[16,3072]{1,0:T(8,128)(2,1)S(1)}, bf16[16,3072]{1,0:T(8,128)(2,1)S(1)}, u32[]{:S(2)}, u32[]{:S(2)}) %collective-permute-start.7) | collective-permute-done | bytes 98336 | tf_op jit(solution)/shard_map/ppermute | solution.py:185
  114.6 0.6 quad.1
  115.2 1.9 %collective-permute-start.13 = (bf16[64,3072]{1,0:T(8,128)(2,1)S(1)}, bf16[64,3072]{1,0:T(8,128)(2,1)S(1)}, u32[]{:S(2)}, u32[]{:S(2)}) collective-permute-start(bf16[64,3072]{1,0:T(8,128)(2,1)S(1)} %get-tuple-element.37.own), channel_id=1, source_target_pairs={{0,15},{1,0},{2,1},{3,2},{4,3},{5,4},{6,5},{7,6},{8,7},{9,8},{10,9... | collective-permute-start | bytes 1179656 | tf_op jit(solution)/shard_map/ppermute | solution.py:185
  117.1 6.6 %collective-permute-start.10 = (bf16[64,3072]{1,0:T(8,128)(2,1)S(1)}, bf16[64,3072]{1,0:T(8,128)(2,1)S(1)}, u32[]{:S(2)}, u32[]{:S(2)}) collective-permute-start(bf16[64,3072]{1,0:T(8,128)(2,1)S(1)} %get-tuple-element.37.own), channel_id=1, source_target_pairs={{0,1},{1,2},{2,3},{3,4},{4,5},{5,6},{6,7},{7,8},{8,9},{9,10},{10,1... | collective-permute-start | bytes 1179656 | tf_op jit(solution)/shard_map/ppermute | solution.py:185
  123.7 3.1 %collective-permute-start.11 = (bf16[64,1536]{1,0:T(8,128)(2,1)S(1)}, bf16[64,1536]{1,0:T(8,128)(2,1)S(1)}, u32[]{:S(2)}, u32[]{:S(2)}) collective-permute-start(bf16[64,1536]{1,0:T(8,128)(2,1)S(1)} %get-tuple-element.38), channel_id=1, source_target_pairs={{0,2},{1,3},{2,4},{3,5},{4,6},{5,7},{6,8},{7,9},{8,10},{9,11},{10,... | collective-permute-start | bytes 589832 | tf_op jit(solution)/shard_map/ppermute | solution.py:185
  126.8 4.3 %collective-permute-start.12 = (bf16[64,1536]{1,0:T(8,128)(2,1)S(1)}, bf16[64,1536]{1,0:T(8,128)(2,1)S(1)}, u32[]{:S(2)}, u32[]{:S(2)}) collective-permute-start(bf16[64,1536]{1,0:T(8,128)(2,1)S(1)} %get-tuple-element.39), channel_id=1, source_target_pairs={{0,14},{1,15},{2,0},{3,1},{4,2},{5,3},{6,4},{7,5},{8,6},{9,7},{10,... | collective-permute-start | bytes 589832 | tf_op jit(solution)/shard_map/ppermute | solution.py:185
  131.1 10.9 %collective-permute-done.11.wa = bf16[64,1536]{1,0:T(8,128)(2,1)S(1)} collective-permute-done((bf16[64,1536]{1,0:T(8,128)(2,1)S(1)}, bf16[64,1536]{1,0:T(8,128)(2,1)S(1)}, u32[]{:S(2)}, u32[]{:S(2)}) %collective-permute-start.11) | collective-permute-done | bytes 196640 | tf_op jit(solution)/shard_map/ppermute | solution.py:185
  141.9 0.0 collective-permute-done.12.wb
  142.0 0.0 collective-permute-done.13.w3
  142.0 2.4 %outputs.1 = (bf16[256,3072]{1,0:T(8,128)(2,1)S(1)}, bf16[256,1024]{1,0:T(8,128)(2,1)}) custom-call(s32[2]{0:T(128)S(1)} %pad_add_fusion.1.place, bf16[64,3072]{1,0:T(8,128)(2,1)S(1)} %get-tuple-element.37.own, bf16[64,3072]{1,0:T(8,128)(2,1)S(1)} %collective-permute-done.10.w1, bf16[64,1536]{1,0:T(8,128)(2,1)S(1)} %collective-permute-done.11.wa, ...), custom_call_target="tpu_custom_call" | custom-call | tf_op jit(solution)/shard_map/outputs/pallas_call | solution.py:17
  144.4 1.2 copy-done.3
  145.6 4.9 %all-to-all-start.1 = ((bf16[32,8,1024]{2,1,0:T(8,128)(2,1)}), bf16[32,8,1024]{2,1,0:T(8,128)(2,1)S(1)}, u32[]{:S(2)}, u32[]{:S(2)}) async-start(bf16[32,8,1024]{2,1,0:T(8,128)(2,1)} %bitcast.9), calls=%async_computation.1 | async-start | bytes 1048576 | tf_op jit(solution)/shard_map/all_to_all | solution.py:239
  150.5 1.4 copy-done.4
  151.9 4.3 %grads.1 = (f32[10,128,128]{2,1,0:T(8,128)}, f32[10,128,128]{2,1,0:T(8,128)}, f32[10,128,128]{2,1,0:T(8,128)}) custom-call(s32[3,10]{1,0:T(4,128)S(1)} %pad_add_fusion.slots, bf16[256,1024]{1,0:T(8,128)(2,1)S(1)} %bitcast.14, bf16[256,3072]{1,0:T(8,128)(2,1)S(1)} %copy-done.4), custom_call_target="tpu_custom_call" | custom-call | tf_op jit(solution)/shard_map/grads/pallas_call | solution.py:17
  156.1 6.0 %all-to-all-done.1.parts = bf16[32,8,1024]{2,1,0:T(8,128)(2,1)S(1)} async-done(((bf16[32,8,1024]{2,1,0:T(8,128)(2,1)}), bf16[32,8,1024]{2,1,0:T(8,128)(2,1)S(1)}, u32[]{:S(2)}, u32[]{:S(2)}) %all-to-all-start.1) | async-done | bytes 524320 | tf_op jit(solution)/shard_map/all_to_all | solution.py:239
  162.2 0.1 row_sum.1
  162.2 0.6 fusion
  (19 shorter events, 0.0 us)
Async XLA Ops:
  0.6 12.1 %copy-start.8 = (s32[1,1,10]{2,1,0:T(1,128)S(1)}, s32[1,1,10]{2,1,0:T(1,128)}, u32[]{:S(2)}) copy-start(s32[1,1,10]{2,1,0:T(1,128)} %param.14) | copy-start | bytes 124
  0.6 12.1 %copy-start.9 = (s32[1,1,10]{2,1,0:T(1,128)S(1)}, s32[1,1,10]{2,1,0:T(1,128)}, u32[]{:S(2)}) copy-start(s32[1,1,10]{2,1,0:T(1,128)} %param.13) | copy-start | bytes 124
  0.7 12.1 %copy-start.10 = (s32[1,1,10]{2,1,0:T(1,128)S(1)}, s32[1,1,10]{2,1,0:T(1,128)}, u32[]{:S(2)}) copy-start(s32[1,1,10]{2,1,0:T(1,128)} %param.12) | copy-start | bytes 124
  0.7 12.1 %copy-start.6 = (bf16[1,1,10,128,128]{4,3,2,1,0:T(8,128)(2,1)S(1)}, bf16[1,1,10,128,128]{4,3,2,1,0:T(8,128)(2,1)}, u32[]{:S(2)}) copy-start(bf16[1,1,10,128,128]{4,3,2,1,0:T(8,128)(2,1)} %param.10) | copy-start | bytes 983044
  0.7 12.1 %copy-start.5 = (bf16[1,1,10,128,128]{4,3,2,1,0:T(8,128)(2,1)S(1)}, bf16[1,1,10,128,128]{4,3,2,1,0:T(8,128)(2,1)}, u32[]{:S(2)}) copy-start(bf16[1,1,10,128,128]{4,3,2,1,0:T(8,128)(2,1)} %param.9) | copy-start | bytes 983044
  2.3 22.1 %all-to-all-start = ((bf16[32,8,1024]{2,1,0:T(8,128)(2,1)}), bf16[32,8,1024]{2,1,0:T(8,128)(2,1)S(1)}, u32[]{:S(2)}, u32[]{:S(2)}) async-start(bf16[32,8,1024]{2,1,0:T(8,128)(2,1)} %broadcast_in_dim.15), calls=%async_computation | async-start | bytes 1048576 | tf_op jit(solution)/shard_map/all_to_all | solution.py:196
  12.8 1.0 copy-start.7
  14.9 1.0 copy-start
  24.4 1.2 copy-start.1
  27.2 114.8 %copy-start.2 = (bf16[1024,512]{1,0:T(8,128)(2,1)S(1)}, bf16[1024,512]{1,0:T(8,128)(2,1)}, u32[]{:S(2)}) copy-start(bf16[1024,512]{1,0:T(8,128)(2,1)} %copy-done) | copy-start | bytes 3145732
  27.2 29.5 %collective-permute-start = (bf16[64,3072]{1,0:T(8,128)(2,1)S(1)}, bf16[64,3072]{1,0:T(8,128)(2,1)S(1)}, u32[]{:S(2)}, u32[]{:S(2)}) collective-permute-start(bf16[64,3072]{1,0:T(8,128)(2,1)S(1)} %get-tuple-element.29), channel_id=1, source_target_pairs={{0,1},{1,2},{2,3},{3,4},{4,5},{5,6},{6,7},{7,8},{8,9},{9,10},{10,1... | collective-permute-start | bytes 1179656 | tf_op jit(solution)/shard_map/ppermute | solution.py:185
  29.2 27.4 %collective-permute-start.1 = (bf16[64,3072]{1,0:T(8,128)(2,1)S(1)}, bf16[64,3072]{1,0:T(8,128)(2,1)S(1)}, u32[]{:S(2)}, u32[]{:S(2)}) collective-permute-start(bf16[64,3072]{1,0:T(8,128)(2,1)S(1)} %get-tuple-element.30), channel_id=1, source_target_pairs={{0,15},{1,0},{2,1},{3,2},{4,3},{5,4},{6,5},{7,6},{8,7},{9,8},{10,9... | collective-permute-start | bytes 1179656 | tf_op jit(solution)/shard_map/ppermute | solution.py:185
  38.5 17.2 %collective-permute-start.2 = (bf16[64,1536]{1,0:T(8,128)(2,1)S(1)}, bf16[64,1536]{1,0:T(8,128)(2,1)S(1)}, u32[]{:S(2)}, u32[]{:S(2)}) collective-permute-start(bf16[64,1536]{1,0:T(8,128)(2,1)S(1)} %get-tuple-element.31), channel_id=1, source_target_pairs={{0,14},{1,15},{2,0},{3,1},{4,2},{5,3},{6,4},{7,5},{8,6},{9,7},{10,... | collective-permute-start | bytes 589832 | tf_op jit(solution)/shard_map/ppermute | solution.py:185
  42.3 14.4 %collective-permute-start.3 = (bf16[64,1536]{1,0:T(8,128)(2,1)S(1)}, bf16[64,1536]{1,0:T(8,128)(2,1)S(1)}, u32[]{:S(2)}, u32[]{:S(2)}) collective-permute-start(bf16[64,1536]{1,0:T(8,128)(2,1)S(1)} %get-tuple-element.32), channel_id=1, source_target_pairs={{0,2},{1,3},{2,4},{3,5},{4,6},{5,7},{6,8},{7,9},{8,10},{9,11},{10,... | collective-permute-start | bytes 589832 | tf_op jit(solution)/shard_map/ppermute | solution.py:185
  57.4 17.5 %collective-permute-start.4 = (bf16[16,3072]{1,0:T(8,128)(2,1)S(1)}, bf16[16,3072]{1,0:T(8,128)(2,1)S(1)}, u32[]{:S(2)}, u32[]{:S(2)}) collective-permute-start(bf16[16,3072]{1,0:T(8,128)(2,1)S(1)} %get-tuple-element.34), channel_id=1, source_target_pairs={{0,4},{1,5},{2,6},{3,7},{4,8},{5,9},{6,10},{7,11},{8,12},{9,13},{1... | collective-permute-start | bytes 294920 | tf_op jit(solution)/shard_map/ppermute | solution.py:185
  61.3 20.5 %collective-permute-start.5 = (bf16[16,3072]{1,0:T(8,128)(2,1)S(1)}, bf16[16,3072]{1,0:T(8,128)(2,1)S(1)}, u32[]{:S(2)}, u32[]{:S(2)}) collective-permute-start(bf16[16,3072]{1,0:T(8,128)(2,1)S(1)} %get-tuple-element.35), channel_id=1, source_target_pairs={{0,8},{1,9},{2,10},{3,11},{4,12},{5,13},{6,14},{7,15},{8,0},{9,1},... | collective-permute-start | bytes 294920 | tf_op jit(solution)/shard_map/ppermute | solution.py:185
  69.7 19.0 %collective-permute-start.6 = (bf16[16,3072]{1,0:T(8,128)(2,1)S(1)}, bf16[16,3072]{1,0:T(8,128)(2,1)S(1)}, u32[]{:S(2)}, u32[]{:S(2)}) collective-permute-start(bf16[16,3072]{1,0:T(8,128)(2,1)S(1)} %get-tuple-element.36), channel_id=1, source_target_pairs={{0,12},{1,13},{2,14},{3,15},{4,0},{5,1},{6,2},{7,3},{8,4},{9,5},{1... | collective-permute-start | bytes 294920 | tf_op jit(solution)/shard_map/ppermute | solution.py:185
  88.8 17.1 %collective-permute-start.9 = (bf16[16,3072]{1,0:T(8,128)(2,1)S(1)}, bf16[16,3072]{1,0:T(8,128)(2,1)S(1)}, u32[]{:S(2)}, u32[]{:S(2)}) collective-permute-start(bf16[16,3072]{1,0:T(8,128)(2,1)S(1)} %hidden.1.own), channel_id=1, source_target_pairs={{0,12},{1,13},{2,14},{3,15},{4,0},{5,1},{6,2},{7,3},{8,4},{9,5},{1... | collective-permute-start | bytes 294920 | tf_op jit(solution)/shard_map/ppermute | solution.py:185
  94.2 16.2 %collective-permute-start.8 = (bf16[16,3072]{1,0:T(8,128)(2,1)S(1)}, bf16[16,3072]{1,0:T(8,128)(2,1)S(1)}, u32[]{:S(2)}, u32[]{:S(2)}) collective-permute-start(bf16[16,3072]{1,0:T(8,128)(2,1)S(1)} %hidden.1.own), channel_id=1, source_target_pairs={{0,8},{1,9},{2,10},{3,11},{4,12},{5,13},{6,14},{7,15},{8,0},{9,1},... | collective-permute-start | bytes 294920 | tf_op jit(solution)/shard_map/ppermute | solution.py:185
  100.0 14.6 %collective-permute-start.7 = (bf16[16,3072]{1,0:T(8,128)(2,1)S(1)}, bf16[16,3072]{1,0:T(8,128)(2,1)S(1)}, u32[]{:S(2)}, u32[]{:S(2)}) collective-permute-start(bf16[16,3072]{1,0:T(8,128)(2,1)S(1)} %hidden.1.own), channel_id=1, source_target_pairs={{0,4},{1,5},{2,6},{3,7},{4,8},{5,9},{6,10},{7,11},{8,12},{9,13},{1... | collective-permute-start | bytes 294920 | tf_op jit(solution)/shard_map/ppermute | solution.py:185
  115.2 26.8 %collective-permute-start.13 = (bf16[64,3072]{1,0:T(8,128)(2,1)S(1)}, bf16[64,3072]{1,0:T(8,128)(2,1)S(1)}, u32[]{:S(2)}, u32[]{:S(2)}) collective-permute-start(bf16[64,3072]{1,0:T(8,128)(2,1)S(1)} %get-tuple-element.37.own), channel_id=1, source_target_pairs={{0,15},{1,0},{2,1},{3,2},{4,3},{5,4},{6,5},{7,6},{8,7},{9,8},{10,9... | collective-permute-start | bytes 1179656 | tf_op jit(solution)/shard_map/ppermute | solution.py:185
  117.1 24.8 %collective-permute-start.10 = (bf16[64,3072]{1,0:T(8,128)(2,1)S(1)}, bf16[64,3072]{1,0:T(8,128)(2,1)S(1)}, u32[]{:S(2)}, u32[]{:S(2)}) collective-permute-start(bf16[64,3072]{1,0:T(8,128)(2,1)S(1)} %get-tuple-element.37.own), channel_id=1, source_target_pairs={{0,1},{1,2},{2,3},{3,4},{4,5},{5,6},{6,7},{7,8},{8,9},{9,10},{10,1... | collective-permute-start | bytes 1179656 | tf_op jit(solution)/shard_map/ppermute | solution.py:185
  123.7 18.3 %collective-permute-start.11 = (bf16[64,1536]{1,0:T(8,128)(2,1)S(1)}, bf16[64,1536]{1,0:T(8,128)(2,1)S(1)}, u32[]{:S(2)}, u32[]{:S(2)}) collective-permute-start(bf16[64,1536]{1,0:T(8,128)(2,1)S(1)} %get-tuple-element.38), channel_id=1, source_target_pairs={{0,2},{1,3},{2,4},{3,5},{4,6},{5,7},{6,8},{7,9},{8,10},{9,11},{10,... | collective-permute-start | bytes 589832 | tf_op jit(solution)/shard_map/ppermute | solution.py:185
  126.8 15.2 %collective-permute-start.12 = (bf16[64,1536]{1,0:T(8,128)(2,1)S(1)}, bf16[64,1536]{1,0:T(8,128)(2,1)S(1)}, u32[]{:S(2)}, u32[]{:S(2)}) collective-permute-start(bf16[64,1536]{1,0:T(8,128)(2,1)S(1)} %get-tuple-element.39), channel_id=1, source_target_pairs={{0,14},{1,15},{2,0},{3,1},{4,2},{5,3},{6,4},{7,5},{8,6},{9,7},{10,... | collective-permute-start | bytes 589832 | tf_op jit(solution)/shard_map/ppermute | solution.py:185
  144.4 1.2 copy-start.3
  145.6 16.6 %all-to-all-start.1 = ((bf16[32,8,1024]{2,1,0:T(8,128)(2,1)}), bf16[32,8,1024]{2,1,0:T(8,128)(2,1)S(1)}, u32[]{:S(2)}, u32[]{:S(2)}) async-start(bf16[32,8,1024]{2,1,0:T(8,128)(2,1)} %bitcast.9), calls=%async_computation.1 | async-start | bytes 1048576 | tf_op jit(solution)/shard_map/all_to_all | solution.py:239
  150.4 1.4 copy-start.4

commit v2 on v1

--- a/solution.py
+++ b/solution.py
@@ -8,6 +8,7 @@
 BLK = 128
 F32 = jnp.float32
 BF16 = jnp.bfloat16
+FLOOR = 2.0**-100
 VMEM_BYTES = 20 * 2**20
 
 
@@ -88,7 +89,7 @@
 
 
 def hidden_kernel(s0, t1, t2, t3, out):
-    hid = out.shape[1] // 3
+    hid = s0.shape[1] // 3
 
     def total(which):
         cols = slice(which * hid, (which + 1) * hid)
@@ -102,31 +103,31 @@
     gate, up, cot = total(0), total(1), total(2)
     sig = jax.nn.sigmoid(gate)
     act = gate * sig
-    out[:, :hid] = (act * up).astype(BF16)
-    out[:, hid : 2 * hid] = (cot * up * (sig * (1.0 + gate * (1.0 - sig)))).astype(BF16)
-    out[:, 2 * hid :] = (cot * act).astype(BF16)
-
-
-def quad_kernel(place, own, v1, v2, v3, whole, low, high):
-    rows = own.shape[0]
-    half = low.shape[1]
-    for off, ref in enumerate((own, v3, v2, v1)):
-        part = at(lax.rem(place[1] + off, 4), rows)
-        whole[part, :] = ref[...]
-        low[part, :] = ref[:, :half]
-        high[part, :] = ref[:, half:]
-
-
-def output_kernel(place, own, w1, wa, wb, w3, gate_w, up_w, down_w, panel, out):
-    rows = own.shape[0]
-    half = wa.shape[1]
+    results = (act * up, cot * up * (sig * (1.0 + gate * (1.0 - sig))), cot * act)
+    rows = out.shape[0]
+    lane = lax.broadcasted_iota(jnp.int32, (rows, BLK), 1)
+    powers = jnp.zeros((rows, BLK), F32)
+    for which, value in enumerate(results):
+        value = value.astype(BF16).astype(F32)
+        most = jnp.max(jnp.abs(value), axis=1, keepdims=True)
+        power = jnp.floor(jnp.log2(jnp.maximum(most, FLOOR)))
+        out[:, which * hid : (which + 1) * hid] = value * jnp.exp2(13.0 - power)
+        powers = jnp.where(lane == which, power, powers)
+    out[:, 3 * hid :] = powers
+
+
+def output_kernel(gathered, gate_w, up_w, down_w, panel, out):
     hid = gate_w.shape[1]
     width = gate_w.shape[0]
-    for off, ref in ((0, own), (1, w3), (3, w1)):
-        panel[at(lax.rem(place[0] + off, 4), rows), :] = ref[...]
-    part = at(lax.rem(place[0] + 2, 4), rows)
-    panel[part, :half] = wa[...]
-    panel[part, half:] = wb[...]
+    share = gathered.shape[0] // 16
+    for dev in range(16):
+        src = slice(dev * share, (dev + 1) * share)
+        dst = (4 * (dev % 4) + dev // 4) * share
+        powers = gathered[src, 3 * hid :].astype(F32)
+        for which in range(3):
+            cols = slice(which * hid, (which + 1) * hid)
+            scale = jnp.exp2(powers[:, which : which + 1] - 13.0)
+            panel[dst : dst + share, cols] = (gathered[src, cols].astype(F32) * scale).astype(BF16)
     out[:, :width] = dot(panel[:, :hid], down_w[...], 1, 0).astype(BF16)
     out[:, width:] = (
         dot(panel[:, hid : 2 * hid], gate_w[...], 1, 1)
@@ -218,21 +219,14 @@
         name="near_sum",
     )
     t1, t3, t2 = shift(s1, 4), shift(s3, -4), shift(s2, 8)
-    (own,) = call(hidden_kernel, (), (s0, t1, t2, t3), (((share, wide), BF16),), name="hidden")
-
-    v1, v3, v2 = shift(own, 4), shift(own, -4), shift(own, 8)
-    whole, low, high = call(
-        quad_kernel,
-        (place,),
-        (own, v1, v2, v3),
-        (((rows, wide), BF16), ((rows, half), BF16), ((rows, half), BF16)),
-        name="quad",
-    )
-    w1, w3, wa, wb = shift(whole, 1), shift(whole, -1), shift(low, 2), shift(high, -2)
+    (own,) = call(
+        hidden_kernel, (), (s0, t1, t2, t3), (((share, wide + BLK), F32),), name="hidden"
+    )
+    gathered = lax.all_gather(own.astype(jnp.float16), "col", axis=0, tiled=True).astype(BF16)
     hidden, out_terms = call(
         output_kernel,
-        (place,),
-        (whole, w1, wa, wb, w3, gate_w, up_w, down_w),
+        (),
+        (gathered, gate_w, up_w, down_w),
         (((count, wide), BF16), ((count, 2 * width), BF16)),
         name="outputs",
     )

time: 164 us -> 147 us (0.90)
  blocking collectives: 0 us -> 30.8 us
  starting transfers between devices: 83.1 us -> 54.8 us
  waiting for transfers between devices: 59.9 us -> 40.2 us
    ppermute x14 -> x7, starting transfers between devices: 67.8 us -> 34.8 us  [shift(): lax.ppermute(value, 'col', [(i, (i + dist) % n_col) for i in range(n_col)])]
    all_gather x0 -> x1, blocking collectives: none -> 30.8 us  [per_device(): lax.all_gather(own.astype(jnp.float16), 'col', axis=0, tiled=True)]
    ppermute x14 -> x7, waiting for transfers between devices: 45.4 us -> 25.8 us  [shift(): lax.ppermute(value, 'col', [(i, (i + dist) % n_col) for i in range(n_col)])]
    all_to_all x1, starting transfers between devices: 4.89 us -> 9.64 us  [per_device(): lax.all_to_all(out_terms.reshape(n_row, local, 2 * width), 'row', 0, 0, t...]
    pallas_call x8 -> x7, Pallas kernels: 10.8 us -> 9.78 us  [call(): pl.pallas_call(kernel, out_shape=[jax.ShapeDtypeStruct(shape, dtype) for...]
  transfers between devices with their start and end apart: 16 -> 9, of which waited for: 9 -> 6; matrix products, arithmetic and copies ran while one was open for 0% -> 0% of each run, Pallas kernels for 3% -> 4%
where the time goes in v2:
time: 147 us; the launch traced here: 146 us
  starting transfers between devices  54.8 us (37%)
  waiting for transfers between devices  40.2 us (27%)
  blocking collectives  30.8 us (21%)
  Pallas kernels  9.78 us (7%)
  local copies, waits for them, and re-layouts  8.3 us (6%)
    ppermute x7, starting transfers between devices, shift(): lax.ppermute(value, 'col', [(i, (i + dist) % n_col) for i in range(n_col)])  34.8 us
    all_gather x1, blocking collectives, per_device(): lax.all_gather(own.astype(jnp.float16), 'col', axis=0, tiled=True)  30.8 us
    ppermute x7, waiting for transfers between devices, shift(): lax.ppermute(value, 'col', [(i, (i + dist) % n_col) for i in range(n_col)])  25.8 us
    all_to_all x1, starting transfers between devices, per_device(): lax.all_to_all(spread, 'row', 0, 0, tiled=True).reshape(count, 2 * width)  10.4 us
    pallas_call x7, Pallas kernels, call(): pl.pallas_call(kernel, out_shape=[jax.ShapeDtypeStruct(shape, dtype) for...  9.78 us
    all_to_all x1, starting transfers between devices, per_device(): lax.all_to_all(out_terms.reshape(n_row, local, 2 * width), 'row', 0, 0, t...  9.64 us
    all_to_all x1, waiting for transfers between devices, per_device(): lax.all_to_all(spread, 'row', 0, 0, tiled=True).reshape(count, 2 * width)  8.43 us
    unnamed x22, local copies, waits for them, and re-layouts  6.83 us
  transfers between devices with their start and end apart: 9, of which 6 were waited for; matrix products, arithmetic and copies ran while one was open for 0% of the time, Pallas kernels for 4%

profile of v2, /device:TPU:1, one launch (start us, length us, event | category | flops | bytes accessed | tf_op | source)
XLA Modules:
  0.0 145.9 jit_solution(11017536215495004971)
XLA Ops:
  0.6 0.0 copy-start.8
  0.6 0.0 copy-start.9
  0.7 0.0 copy-start.10
  0.7 0.0 copy-start.6
  0.7 0.0 copy-start.5
  0.7 0.8 pad_maximum_fusion
  1.5 0.9 broadcast_in_dim.15
  2.3 10.4 %all-to-all-start = ((bf16[32,8,1024]{2,1,0:T(8,128)(2,1)}), bf16[32,8,1024]{2,1,0:T(8,128)(2,1)S(1)}, u32[]{:S(2)}, u32[]{:S(2)}) async-start(bf16[32,8,1024]{2,1,0:T(8,128)(2,1)} %broadcast_in_dim.15), calls=%async_computation | async-start | bytes 1048576 | tf_op jit(solution)/shard_map/all_to_all | solution.py:197
  12.7 0.0 copy-done.8
  12.7 0.0 copy-done.9
  12.8 0.0 copy-done.10
  12.8 0.0 copy-done.6
  12.8 0.0 copy-start.7
  12.8 1.0 copy-done.7
  13.8 1.1 place.1
  14.9 1.0 copy-done
  15.9 0.1 pad_add_fusion.1.place
  16.0 8.4 %all-to-all-done = bf16[32,8,1024]{2,1,0:T(8,128)(2,1)S(1)} async-done(((bf16[32,8,1024]{2,1,0:T(8,128)(2,1)}), bf16[32,8,1024]{2,1,0:T(8,128)(2,1)S(1)}, u32[]{:S(2)}, u32[]{:S(2)}) %all-to-all-start) | async-done | bytes 524320 | tf_op jit(solution)/shard_map/all_to_all | solution.py:197
  24.4 1.2 copy-done.1
  25.6 1.5 %partials.1 = (bf16[64,3072]{1,0:T(8,128)(2,1)S(1)}, bf16[64,3072]{1,0:T(8,128)(2,1)S(1)}, bf16[64,1536]{1,0:T(8,128)(2,1)S(1)}, bf16[64,1536]{1,0:T(8,128)(2,1)S(1)}, bf16[64,3072]{1,0:T(8,128)(2,1)S(1)}) custom-call(s32[2]{0:T(128)S(1)} %pad_add_fusion.1.place, bf16[256,1024]{1,0:T(8,128)(2,1)S(1)} %bitcast.13, ...), custom_call_target="tpu_custom_call" | custom-call | tf_op jit(solution)/shard_map/partials/pallas_call | solution.py:18
  27.2 1.9 %collective-permute-start = (bf16[64,3072]{1,0:T(8,128)(2,1)S(1)}, bf16[64,3072]{1,0:T(8,128)(2,1)S(1)}, u32[]{:S(2)}, u32[]{:S(2)}) collective-permute-start(bf16[64,3072]{1,0:T(8,128)(2,1)S(1)} %get-tuple-element.26), channel_id=1, source_target_pairs={{0,1},{1,2},{2,3},{3,4},{4,5},{5,6},{6,7},{7,8},{8,9},{9,10},{10,1... | collective-permute-start | bytes 1179656 | tf_op jit(solution)/shard_map/ppermute | solution.py:186
  29.1 9.2 %collective-permute-start.1 = (bf16[64,3072]{1,0:T(8,128)(2,1)S(1)}, bf16[64,3072]{1,0:T(8,128)(2,1)S(1)}, u32[]{:S(2)}, u32[]{:S(2)}) collective-permute-start(bf16[64,3072]{1,0:T(8,128)(2,1)S(1)} %get-tuple-element.27), channel_id=1, source_target_pairs={{0,15},{1,0},{2,1},{3,2},{4,3},{5,4},{6,5},{7,6},{8,7},{9,8},{10,9... | collective-permute-start | bytes 1179656 | tf_op jit(solution)/shard_map/ppermute | solution.py:186
  38.3 3.8 %collective-permute-start.2 = (bf16[64,1536]{1,0:T(8,128)(2,1)S(1)}, bf16[64,1536]{1,0:T(8,128)(2,1)S(1)}, u32[]{:S(2)}, u32[]{:S(2)}) collective-permute-start(bf16[64,1536]{1,0:T(8,128)(2,1)S(1)} %get-tuple-element.28), channel_id=1, source_target_pairs={{0,14},{1,15},{2,0},{3,1},{4,2},{5,3},{6,4},{7,5},{8,6},{9,7},{10,... | collective-permute-start | bytes 589832 | tf_op jit(solution)/shard_map/ppermute | solution.py:186
  42.1 2.4 %collective-permute-start.3 = (bf16[64,1536]{1,0:T(8,128)(2,1)S(1)}, bf16[64,1536]{1,0:T(8,128)(2,1)S(1)}, u32[]{:S(2)}, u32[]{:S(2)}) collective-permute-start(bf16[64,1536]{1,0:T(8,128)(2,1)S(1)} %get-tuple-element.29), channel_id=1, source_target_pairs={{0,2},{1,3},{2,4},{3,5},{4,6},{5,7},{6,8},{7,9},{8,10},{9,11},{10,... | collective-permute-start | bytes 589832 | tf_op jit(solution)/shard_map/ppermute | solution.py:186
  44.5 11.0 %collective-permute-done.2.ra = bf16[64,1536]{1,0:T(8,128)(2,1)S(1)} collective-permute-done((bf16[64,1536]{1,0:T(8,128)(2,1)S(1)}, bf16[64,1536]{1,0:T(8,128)(2,1)S(1)}, u32[]{:S(2)}, u32[]{:S(2)}) %collective-permute-start.2) | collective-permute-done | bytes 196640 | tf_op jit(solution)/shard_map/ppermute | solution.py:186
  55.5 1.0 collective-permute-done.3.rb
  56.5 0.0 collective-permute-done.r1
  56.5 0.0 collective-permute-done.1.r3
  56.5 0.7 near_sum.1
  57.3 3.9 %collective-permute-start.4 = (bf16[16,3072]{1,0:T(8,128)(2,1)S(1)}, bf16[16,3072]{1,0:T(8,128)(2,1)S(1)}, u32[]{:S(2)}, u32[]{:S(2)}) collective-permute-start(bf16[16,3072]{1,0:T(8,128)(2,1)S(1)} %get-tuple-element.31), channel_id=1, source_target_pairs={{0,4},{1,5},{2,6},{3,7},{4,8},{5,9},{6,10},{7,11},{8,12},{9,13},{1... | collective-permute-start | bytes 294920 | tf_op jit(solution)/shard_map/ppermute | solution.py:186
  61.2 8.4 %collective-permute-start.5 = (bf16[16,3072]{1,0:T(8,128)(2,1)S(1)}, bf16[16,3072]{1,0:T(8,128)(2,1)S(1)}, u32[]{:S(2)}, u32[]{:S(2)}) collective-permute-start(bf16[16,3072]{1,0:T(8,128)(2,1)S(1)} %get-tuple-element.32), channel_id=1, source_target_pairs={{0,8},{1,9},{2,10},{3,11},{4,12},{5,13},{6,14},{7,15},{8,0},{9,1},... | collective-permute-start | bytes 294920 | tf_op jit(solution)/shard_map/ppermute | solution.py:186
  69.6 5.2 %collective-permute-start.6 = (bf16[16,3072]{1,0:T(8,128)(2,1)S(1)}, bf16[16,3072]{1,0:T(8,128)(2,1)S(1)}, u32[]{:S(2)}, u32[]{:S(2)}) collective-permute-start(bf16[16,3072]{1,0:T(8,128)(2,1)S(1)} %get-tuple-element.33), channel_id=1, source_target_pairs={{0,12},{1,13},{2,14},{3,15},{4,0},{5,1},{6,2},{7,3},{8,4},{9,5},{1... | collective-permute-start | bytes 294920 | tf_op jit(solution)/shard_map/ppermute | solution.py:186
  74.8 0.0 collective-permute-done.4.t1
  74.8 6.8 %collective-permute-done.5.t2 = bf16[16,3072]{1,0:T(8,128)(2,1)S(1)} collective-permute-done((bf16[16,3072]{1,0:T(8,128)(2,1)S(1)}, bf16[16,3072]{1,0:T(8,128)(2,1)S(1)}, u32[]{:S(2)}, u32[]{:S(2)}) %collective-permute-start.5) | collective-permute-done | bytes 98336 | tf_op jit(solution)/shard_map/ppermute | solution.py:186
  81.6 6.9 %collective-permute-done.6.t3 = bf16[16,3072]{1,0:T(8,128)(2,1)S(1)} collective-permute-done((bf16[16,3072]{1,0:T(8,128)(2,1)S(1)}, bf16[16,3072]{1,0:T(8,128)(2,1)S(1)}, u32[]{:S(2)}, u32[]{:S(2)}) %collective-permute-start.6) | collective-permute-done | bytes 98336 | tf_op jit(solution)/shard_map/ppermute | solution.py:186
  88.6 0.2 hidden.1
  88.8 30.8 %all-gather.1 = f16[256,3200]{1,0:T(8,128)(2,1)S(1)} all-gather(f16[16,3200]{1,0:T(8,128)(2,1)S(1)} %convert_element_type.6), channel_id=1, replica_groups=mesh['row'=32,'col'=16] {'col'}, dimensions={0}, use_global_device_ids=true | all-gather | bytes 1740800 | tf_op jit(solution)/shard_map/all_gather | solution.py:225
  119.6 0.2 convert_element_type.7.gathered
  119.8 1.0 copy-done.2
  120.8 1.9 %outputs.1 = (bf16[256,3072]{1,0:T(8,128)(2,1)S(1)}, bf16[256,1024]{1,0:T(8,128)(2,1)}) custom-call(bf16[256,3200]{1,0:T(8,128)(2,1)S(1)} %convert_element_type.7.gathered, bf16[512,1024]{1,0:T(8,128)(2,1)S(1)} %get-tuple-element.22.gate_w, bf16[512,1024]{1,0:T(8,128)(2,1)S(1)} %get-tuple-element.23.up_w, bf16[1024,512]{1,0:T(8,128)(2,1)S(1)} %copy-done.2), custom_call_target="tpu_custom_call" | custom-call | tf_op jit(solution)/shard_map/outputs/pallas_call | solution.py:18
  122.7 1.2 copy-done.3
  123.9 9.6 %all-to-all-start.1 = ((bf16[32,8,1024]{2,1,0:T(8,128)(2,1)}), bf16[32,8,1024]{2,1,0:T(8,128)(2,1)S(1)}, u32[]{:S(2)}, u32[]{:S(2)}) async-start(bf16[32,8,1024]{2,1,0:T(8,128)(2,1)} %bitcast.9), calls=%async_computation.1 | async-start | bytes 1048576 | tf_op jit(solution)/shard_map/all_to_all | solution.py:233
  133.5 0.0 copy-start.4
  133.5 1.4 copy-done.4
  134.9 4.3 %grads.1 = (f32[10,128,128]{2,1,0:T(8,128)}, f32[10,128,128]{2,1,0:T(8,128)}, f32[10,128,128]{2,1,0:T(8,128)}) custom-call(s32[3,10]{1,0:T(4,128)S(1)} %pad_add_fusion.slots, bf16[256,1024]{1,0:T(8,128)(2,1)S(1)} %bitcast.14, bf16[256,3072]{1,0:T(8,128)(2,1)S(1)} %copy-done.4), custom_call_target="tpu_custom_call" | custom-call | tf_op jit(solution)/shard_map/grads/pallas_call | solution.py:18
  139.2 6.0 %all-to-all-done.1.parts = bf16[32,8,1024]{2,1,0:T(8,128)(2,1)S(1)} async-done(((bf16[32,8,1024]{2,1,0:T(8,128)(2,1)}), bf16[32,8,1024]{2,1,0:T(8,128)(2,1)S(1)}, u32[]{:S(2)}, u32[]{:S(2)}) %all-to-all-start.1) | async-done | bytes 524320 | tf_op jit(solution)/shard_map/all_to_all | solution.py:233
  145.2 0.1 row_sum.1
  145.3 0.6 fusion
  (7 shorter events, 0.0 us)
Async XLA Ops:
  0.6 12.1 %copy-start.8 = (s32[1,1,10]{2,1,0:T(1,128)S(1)}, s32[1,1,10]{2,1,0:T(1,128)}, u32[]{:S(2)}) copy-start(s32[1,1,10]{2,1,0:T(1,128)} %param.14) | copy-start | bytes 124
  0.6 12.1 %copy-start.9 = (s32[1,1,10]{2,1,0:T(1,128)S(1)}, s32[1,1,10]{2,1,0:T(1,128)}, u32[]{:S(2)}) copy-start(s32[1,1,10]{2,1,0:T(1,128)} %param.13) | copy-start | bytes 124
  0.7 12.1 %copy-start.10 = (s32[1,1,10]{2,1,0:T(1,128)S(1)}, s32[1,1,10]{2,1,0:T(1,128)}, u32[]{:S(2)}) copy-start(s32[1,1,10]{2,1,0:T(1,128)} %param.12) | copy-start | bytes 124
  0.7 12.1 %copy-start.6 = (bf16[1,1,10,128,128]{4,3,2,1,0:T(8,128)(2,1)S(1)}, bf16[1,1,10,128,128]{4,3,2,1,0:T(8,128)(2,1)}, u32[]{:S(2)}) copy-start(bf16[1,1,10,128,128]{4,3,2,1,0:T(8,128)(2,1)} %param.10) | copy-start | bytes 983044
  0.7 12.1 %copy-start.5 = (bf16[1,1,10,128,128]{4,3,2,1,0:T(8,128)(2,1)S(1)}, bf16[1,1,10,128,128]{4,3,2,1,0:T(8,128)(2,1)}, u32[]{:S(2)}) copy-start(bf16[1,1,10,128,128]{4,3,2,1,0:T(8,128)(2,1)} %param.9) | copy-start | bytes 983044
  2.3 22.1 %all-to-all-start = ((bf16[32,8,1024]{2,1,0:T(8,128)(2,1)}), bf16[32,8,1024]{2,1,0:T(8,128)(2,1)S(1)}, u32[]{:S(2)}, u32[]{:S(2)}) async-start(bf16[32,8,1024]{2,1,0:T(8,128)(2,1)} %broadcast_in_dim.15), calls=%async_computation | async-start | bytes 1048576 | tf_op jit(solution)/shard_map/all_to_all | solution.py:197
  12.8 1.0 copy-start.7
  14.9 1.0 copy-start
  24.4 1.2 copy-start.1
  27.2 29.3 %collective-permute-start = (bf16[64,3072]{1,0:T(8,128)(2,1)S(1)}, bf16[64,3072]{1,0:T(8,128)(2,1)S(1)}, u32[]{:S(2)}, u32[]{:S(2)}) collective-permute-start(bf16[64,3072]{1,0:T(8,128)(2,1)S(1)} %get-tuple-element.26), channel_id=1, source_target_pairs={{0,1},{1,2},{2,3},{3,4},{4,5},{5,6},{6,7},{7,8},{8,9},{9,10},{10,1... | collective-permute-start | bytes 1179656 | tf_op jit(solution)/shard_map/ppermute | solution.py:186
  29.1 27.4 %collective-permute-start.1 = (bf16[64,3072]{1,0:T(8,128)(2,1)S(1)}, bf16[64,3072]{1,0:T(8,128)(2,1)S(1)}, u32[]{:S(2)}, u32[]{:S(2)}) collective-permute-start(bf16[64,3072]{1,0:T(8,128)(2,1)S(1)} %get-tuple-element.27), channel_id=1, source_target_pairs={{0,15},{1,0},{2,1},{3,2},{4,3},{5,4},{6,5},{7,6},{8,7},{9,8},{10,9... | collective-permute-start | bytes 1179656 | tf_op jit(solution)/shard_map/ppermute | solution.py:186
  38.3 17.2 %collective-permute-start.2 = (bf16[64,1536]{1,0:T(8,128)(2,1)S(1)}, bf16[64,1536]{1,0:T(8,128)(2,1)S(1)}, u32[]{:S(2)}, u32[]{:S(2)}) collective-permute-start(bf16[64,1536]{1,0:T(8,128)(2,1)S(1)} %get-tuple-element.28), channel_id=1, source_target_pairs={{0,14},{1,15},{2,0},{3,1},{4,2},{5,3},{6,4},{7,5},{8,6},{9,7},{10,... | collective-permute-start | bytes 589832 | tf_op jit(solution)/shard_map/ppermute | solution.py:186
  42.1 14.4 %collective-permute-start.3 = (bf16[64,1536]{1,0:T(8,128)(2,1)S(1)}, bf16[64,1536]{1,0:T(8,128)(2,1)S(1)}, u32[]{:S(2)}, u32[]{:S(2)}) collective-permute-start(bf16[64,1536]{1,0:T(8,128)(2,1)S(1)} %get-tuple-element.29), channel_id=1, source_target_pairs={{0,2},{1,3},{2,4},{3,5},{4,6},{5,7},{6,8},{7,9},{8,10},{9,11},{10,... | collective-permute-start | bytes 589832 | tf_op jit(solution)/shard_map/ppermute | solution.py:186
  57.3 17.5 %collective-permute-start.4 = (bf16[16,3072]{1,0:T(8,128)(2,1)S(1)}, bf16[16,3072]{1,0:T(8,128)(2,1)S(1)}, u32[]{:S(2)}, u32[]{:S(2)}) collective-permute-start(bf16[16,3072]{1,0:T(8,128)(2,1)S(1)} %get-tuple-element.31), channel_id=1, source_target_pairs={{0,4},{1,5},{2,6},{3,7},{4,8},{5,9},{6,10},{7,11},{8,12},{9,13},{1... | collective-permute-start | bytes 294920 | tf_op jit(solution)/shard_map/ppermute | solution.py:186
  61.2 20.5 %collective-permute-start.5 = (bf16[16,3072]{1,0:T(8,128)(2,1)S(1)}, bf16[16,3072]{1,0:T(8,128)(2,1)S(1)}, u32[]{:S(2)}, u32[]{:S(2)}) collective-permute-start(bf16[16,3072]{1,0:T(8,128)(2,1)S(1)} %get-tuple-element.32), channel_id=1, source_target_pairs={{0,8},{1,9},{2,10},{3,11},{4,12},{5,13},{6,14},{7,15},{8,0},{9,1},... | collective-permute-start | bytes 294920 | tf_op jit(solution)/shard_map/ppermute | solution.py:186
  69.6 19.0 %collective-permute-start.6 = (bf16[16,3072]{1,0:T(8,128)(2,1)S(1)}, bf16[16,3072]{1,0:T(8,128)(2,1)S(1)}, u32[]{:S(2)}, u32[]{:S(2)}) collective-permute-start(bf16[16,3072]{1,0:T(8,128)(2,1)S(1)} %get-tuple-element.33), channel_id=1, source_target_pairs={{0,12},{1,13},{2,14},{3,15},{4,0},{5,1},{6,2},{7,3},{8,4},{9,5},{1... | collective-permute-start | bytes 294920 | tf_op jit(solution)/shard_map/ppermute | solution.py:186
  119.6 1.2 copy-start.2
  122.7 1.2 copy-start.3
  123.9 21.4 %all-to-all-start.1 = ((bf16[32,8,1024]{2,1,0:T(8,128)(2,1)}), bf16[32,8,1024]{2,1,0:T(8,128)(2,1)S(1)}, u32[]{:S(2)}, u32[]{:S(2)}) async-start(bf16[32,8,1024]{2,1,0:T(8,128)(2,1)} %bitcast.9), calls=%async_computation.1 | async-start | bytes 1048576 | tf_op jit(solution)/shard_map/all_to_all | solution.py:233
  133.5 1.4 copy-start.4

commit v3 on v2

v3 whole, which is shorter than its diff:
```python
import jax
import jax.numpy as jnp
import numpy as np
from jax import lax
from jax.experimental import pallas as pl
from jax.experimental.pallas import tpu as pltpu
from jax.sharding import PartitionSpec as P

BLK = 128
F32 = jnp.float32
BF16 = jnp.bfloat16
FLOOR = 2.0**-100
VMEM_BYTES = 20 * 2**20


def call(kernel, scalars, arrays, outs, scratch=(), name=None, far=(), far_outs=()):
    arrays = [
        pltpu.with_memory_space_constraint(array, pltpu.HBM) if i in far else array
        for i, array in enumerate(arrays)
    ]
    in_specs = [pl.BlockSpec(memory_space=pltpu.SMEM) for _ in scalars]
    in_specs += [
        pl.BlockSpec(memory_space=pltpu.HBM if i in far else pltpu.VMEM)
        for i in range(len(arrays))
    ]
    return pl.pallas_call(
        kernel,
        out_shape=[
            pltpu.HBM(*out) if i in far_outs else jax.ShapeDtypeStruct(*out)
            for i, out in enumerate(outs)
        ],
        in_specs=in_specs,
        out_specs=[
            pl.BlockSpec(memory_space=pltpu.HBM if i in far_outs else pltpu.VMEM)
            for i in range(len(outs))
        ],
        scratch_shapes=list(scratch),
        compiler_params=pltpu.CompilerParams(vmem_limit_bytes=VMEM_BYTES),
        name=name,
    )(*scalars, *arrays)


def at(index, size):
    return pl.ds(pl.multiple_of(index * size, size), size)


def dot(left, right, left_dim, right_dim):
    return lax.dot_general(
        left, right, (((left_dim,), (right_dim,)), ((), ())), preferred_element_type=F32
    )


def spread_kernel(tokens, grads, out):
    width = tokens.shape[1]
    out[:, :, :width] = jnp.broadcast_to(tokens[...][None], (out.shape[0],) + tokens.shape)
    out[:, :, width:] = jnp.broadcast_to(grads[...][None], (out.shape[0],) + grads.shape)


def place_kernel(
    slots, gate_blk, up_blk, down_blk, gate_ref, up_out, down_out, up_ref, down_ref, sems
):
    tiles = ((down_blk, down_ref, 2), (up_blk, up_ref, 1), (gate_blk, gate_ref, 0))
    copies = {
        1: pltpu.make_async_copy(up_ref, up_out, sems.at[0]),
        2: pltpu.make_async_copy(down_ref, down_out, sems.at[1]),
    }
    for blk, ref, which in tiles:
        ref[...] = jnp.zeros_like(ref)
        col_blocks = ref.shape[1] // BLK
        total = (ref.shape[0] // BLK) * col_blocks
        for slot in range(blk.shape[0]):
            number = slots[which, slot]

            @pl.when(number < total)
            def _(number=number, slot=slot, blk=blk, ref=ref, col_blocks=col_blocks):
                ref[at(number // col_blocks, BLK), at(number % col_blocks, BLK)] = blk[slot]

        if which > 0:
            copies[which].start()
    copies[1].wait()
    copies[2].wait()


def row_moves(share, n_col):
    keep = share - 1
    rows = np.zeros((n_col * keep, n_col * share), np.float32)
    last = np.zeros((n_col, n_col * share), np.float32)
    spot = np.zeros((n_col * keep, 8 * n_col), np.float32)
    for dev in range(n_col):
        last[dev, dev * share + keep] = 1.0
        for row in range(keep):
            rows[dev * keep + row, dev * share + row] = 1.0
        for blk in range(8):
            spot[dev * keep + blk, blk * n_col + dev] = 1.0
    return tuple(jnp.asarray(m, BF16) for m in (rows, last, spot))


def partial_kernel(panel, gate_w, rows, last, spot, up_far, down_far, out, up_w, down_w, sems):
    copies = {
        1: pltpu.make_async_copy(up_far, up_w, sems.at[0]),
        2: pltpu.make_async_copy(down_far, down_w, sems.at[1]),
    }
    copies[1].start()
    copies[2].start()
    width, hid = gate_w.shape
    main = dot(rows[...], panel[...], 1, 0).astype(BF16)
    ends = dot(last[...], panel[...], 1, 0).astype(BF16)
    jobs = ((0, gate_w, 0), (0, up_w, 0), (width, down_w, 1))
    for which, (lo, weight, dim) in enumerate(jobs):
        if which > 0:
            copies[which].wait()
        base = which * (hid + BLK)
        tile = weight[...]
        out[:, base : base + hid] = dot(main[:, lo : lo + width], tile, 1, dim).astype(BF16)
        end = dot(ends[:, lo : lo + width], tile, 1, dim).astype(BF16)
        pieces = [end[:, blk * BLK : (blk + 1) * BLK] for blk in range(hid // BLK)]
        moved = dot(spot[...], jnp.concatenate(pieces, axis=0), 1, 0)
        out[:, base + hid : base + hid + BLK] = moved.astype(BF16)


def hidden_kernel(sums, out, full):
    keep = sums.shape[0]
    step = sums.shape[1] // 3
    hid = step - BLK
    gate, up, cot = (sums[:, i * step : (i + 1) * step].astype(F32) for i in range(3))
    sig = jax.nn.sigmoid(gate)
    act = gate * sig
    results = (act * up, cot * up * (sig * (1.0 + gate * (1.0 - sig))), cot * act)
    lane = lax.broadcasted_iota(jnp.int32, (keep + 1, BLK), 1)
    powers = jnp.zeros((keep + 1, BLK), F32)
    for which, value in enumerate(results):
        value = value.astype(BF16).astype(F32)
        full[0:keep, :] = value[:, :hid]
        for blk in range(hid // BLK):
            full[keep : keep + 1, blk * BLK : (blk + 1) * BLK] = value[blk : blk + 1, hid:]
        value = full[...]
        most = jnp.max(jnp.abs(value), axis=1, keepdims=True)
        power = jnp.floor(jnp.log2(jnp.maximum(most, FLOOR)))
        out[:, which * hid : (which + 1) * hid] = value * jnp.exp2(13.0 - power)
        powers = jnp.where(lane == which, power, powers)
    out[:, 3 * hid :] = powers


def output_kernel(
    gathered, gate_w, up_far, down_far, panel_out, out, panel, up_w, down_w, sems
):
    load_up = pltpu.make_async_copy(up_far, up_w, sems.at[0])
    load = pltpu.make_async_copy(down_far, down_w, sems.at[1])
    store = pltpu.make_async_copy(panel, panel_out, sems.at[2])
    load_up.start()
    load.start()
    width, hid = gate_w.shape
    powers = gathered[:, 3 * hid :].astype(F32)
    for which in range(3):
        cols = slice(which * hid, (which + 1) * hid)
        scale = jnp.exp2(powers[:, which : which + 1] - 13.0)
        panel[:, cols] = (gathered[:, cols].astype(F32) * scale).astype(BF16)
    store.start()
    load_up.wait()
    out[:, width:] = (
        dot(panel[:, hid : 2 * hid], gate_w[...], 1, 1)
        + dot(panel[:, 2 * hid :], up_w[...], 1, 1)
    ).astype(BF16)
    load.wait()
    out[:, :width] = dot(panel[:, :hid], down_w[...], 1, 0).astype(BF16)
    store.wait()


def grad_kernel(slots, panel, hidden, gate_out, up_out, down_out, act_t, hid_t):
    width = panel.shape[1] // 2
    hid = hidden.shape[1] // 3
    for blk in range(width // BLK):
        act_t[blk] = panel[:, blk * BLK : (blk + 1) * BLK].T
    for blk in range(hid // BLK):
        hid_t[blk] = hidden[:, blk * BLK : (blk + 1) * BLK].T
    jobs = (
        (act_t, hidden, hid, hid // BLK, gate_out),
        (act_t, hidden, 2 * hid, hid // BLK, up_out),
        (hid_t, panel, width, width // BLK, down_out),
    )
    for which, (left, right, base, col_blocks, out) in enumerate(jobs):
        total = left.shape[0] * col_blocks
        for slot in range(out.shape[0]):
            number = slots[which, slot]
            live = number < total

            @pl.when(live)
            def _(number=number, slot=slot, left=left, right=right, base=base, out=out, n=col_blocks):
                cols = at(base // BLK + number % n, BLK)
                out[slot] = dot(left[number // n], right[:, cols], 1, 0)

            @pl.when(jnp.logical_not(live))
            def _(slot=slot, out=out):
                out[slot] = jnp.zeros(out.shape[1:], F32)


def sum_kernel(parts, first, second):
    total = jnp.sum(parts[...].astype(F32), axis=0).astype(BF16)
    first[...] = total[:, : first.shape[1]]
    second[...] = total[:, first.shape[1] :]


def per_device(
    tokens, gate_blocks, up_blocks, down_blocks, gate_slots, up_slots, down_slots, out_grad
):
    n_row, n_col = lax.axis_size("row"), lax.axis_size("col")
    local, width = tokens.shape
    count = local * n_row
    share = count // n_col
    hid = 8 * BLK
    wide = 3 * hid
    slots = jnp.stack([gate_slots[0, 0], up_slots[0, 0], down_slots[0, 0]])

    gate_w, up_w, down_w = call(
        place_kernel,
        (slots,),
        (gate_blocks[0, 0], up_blocks[0, 0], down_blocks[0, 0]),
        (((width, hid), BF16), ((width, hid), BF16), ((hid, width), BF16)),
        (
            pltpu.VMEM((width, hid), BF16),
            pltpu.VMEM((hid, width), BF16),
            pltpu.SemaphoreType.DMA((2,)),
        ),
        name="place",
        far_outs=(1, 2),
    )
    (spread,) = call(
        spread_kernel, (), (tokens, out_grad), (((n_row, local, 2 * width), BF16),), name="spread"
    )
    panel = lax.all_to_all(spread, "row", 0, 0, tiled=True).reshape(count, 2 * width)

    (terms,) = call(
        partial_kernel,
        (),
        (panel, gate_w) + row_moves(share, n_col) + (up_w, down_w),
        (((n_col * (share - 1), wide + 3 * BLK), BF16),),
        (
            pltpu.VMEM((width, hid), BF16),
            pltpu.VMEM((hid, width), BF16),
            pltpu.SemaphoreType.DMA((2,)),
        ),
        name="partials",
        far=(5, 6),
    )
    sums = lax.psum_scatter(terms, "col", scatter_dimension=0, tiled=True)
    (own,) = call(
        hidden_kernel,
        (),
        (sums,),
        (((share, wide + BLK), F32),),
        (pltpu.VMEM((share, hid), F32),),
        name="hidden",
    )
    gathered = lax.all_gather(own.astype(jnp.float16), "col", axis=0, tiled=True).astype(BF16)
    hidden, out_terms = call(
        output_kernel,
        (),
        (gathered, gate_w, up_w, down_w),
        (((count, wide), BF16), ((count, 2 * width), BF16)),
        (
            pltpu.VMEM((count, wide), BF16),
            pltpu.VMEM((width, hid), BF16),
            pltpu.VMEM((hid, width), BF16),
            pltpu.SemaphoreType.DMA((3,)),
        ),
        name="outputs",
        far=(2, 3),
        far_outs=(0,),
    )
    parts = lax.all_to_all(
        out_terms.reshape(n_row, local, 2 * width), "row", 0, 0, tiled=True
    )
    gate_grad, up_grad, down_grad = call(
        grad_kernel,
        (slots,),
        (panel, hidden),
        tuple((ref.shape[2:], F32) for ref in (gate_blocks, up_blocks, down_blocks)),
        (
            pltpu.VMEM((width // BLK, BLK, count), BF16),
            pltpu.VMEM((hid // BLK, BLK, count), BF16),
        ),
        name="grads",
    )
    layer_out, token_grad = call(
        sum_kernel, (), (parts,), (((local, width), BF16),) * 2, name="row_sum"
    )
    return (
        layer_out,
        token_grad,
        gate_grad[None, None],
        up_grad[None, None],
        down_grad[None, None],
    )


def solution(mesh):
    in_specs = (
        P("row", "col"),
        P("col", "row", None, None, None),
        P("col", "row", None, None, None),
        P("row", "col", None, None, None),
        P("col", "row", None),
        P("col", "row", None),
        P("row", "col", None),
        P("row", "col"),
    )
    out_specs = (
        P("row", "col"),
        P("row", "col"),
        P("col", "row", None, None, None),
        P("col", "row", None, None, None),
        P("row", "col", None, None, None),
    )
    return jax.shard_map(
        per_device, mesh=mesh, in_specs=in_specs, out_specs=out_specs, check_vma=False
    )
```

time: 147 us -> 139 us (0.946)
  blocking collectives: 30.8 us -> 72 us
  waiting for transfers between devices: 40.2 us -> 15 us
  starting transfers between devices: 54.8 us -> 29.9 us
  Pallas kernels: 9.78 us -> 14.5 us
  local copies, waits for them, and re-layouts: 8.3 us -> 4.57 us
    unnamed x0 -> x1, blocking collectives: none -> 38 us
    ppermute x7 -> x0, starting transfers between devices: 34.8 us -> none  [shift(): lax.ppermute(value, 'col', [(i, (i + dist) % n_col) for i in range(n_col)])]
    ppermute x7 -> x0, waiting for transfers between devices: 25.8 us -> none  [shift(): lax.ppermute(value, 'col', [(i, (i + dist) % n_col) for i in range(n_col)])]
    all_to_all x1, starting transfers between devices: 9.64 us -> 16.7 us  [per_device(): lax.all_to_all(out_terms.reshape(n_row, local, 2 * width), 'row', 0, 0, t...]
    pallas_call x7, Pallas kernels: 9.78 us -> 14.5 us  [call(): pl.pallas_call(kernel, out_shape=[pltpu.HBM(*out) if i in far_outs else j...]
    all_gather x1, blocking collectives: 30.8 us -> 34 us  [per_device(): lax.all_gather(own.astype(jnp.float16), 'col', axis=0, tiled=True)]
    unnamed x0 -> x1, starting transfers between devices: none -> 2.87 us
    unnamed x22, local copies, waits for them, and re-layouts: 6.83 us -> 4.57 us
  transfers between devices with their start and end apart: 9 -> 3, of which waited for: 6 -> 2; matrix products, arithmetic and copies ran while one was open for 0% -> 1% of each run, Pallas kernels for 4% -> 4%
where the time goes in v3:
time: 139 us; the launch traced here: 138 us
  blocking collectives  72 us (52%)
  starting transfers between devices  29.9 us (22%)
  waiting for transfers between devices  15 us (11%)
  Pallas kernels  14.5 us (10%)
  local copies, waits for them, and re-layouts  4.57 us (3%)
  between operations  1.46 us (1%)
    unnamed x1, blocking collectives  38 us
    all_gather x1, blocking collectives, per_device(): lax.all_gather(own.astype(jnp.float16), 'col', axis=0, tiled=True)  34 us
    all_to_all x1, starting transfers between devices, per_device(): lax.all_to_all(out_terms.reshape(n_row, local, 2 * width), 'row', 0, 0, t...  16.7 us
    pallas_call x7, Pallas kernels, call(): pl.pallas_call(kernel, out_shape=[pltpu.HBM(*out) if i in far_outs else j...  14.5 us
    all_to_all x1, starting transfers between devices, per_device(): lax.all_to_all(spread, 'row', 0, 0, tiled=True).reshape(count, 2 * width)  10.4 us
    all_to_all x1, waiting for transfers between devices, per_device(): lax.all_to_all(spread, 'row', 0, 0, tiled=True).reshape(count, 2 * width)  8.9 us
    all_to_all x1, waiting for transfers between devices, per_device(): lax.all_to_all(out_terms.reshape(n_row, local, 2 * width), 'row', 0, 0, t...  6.08 us
    unnamed x22, local copies, waits for them, and re-layouts  4.57 us
  transfers between devices with their start and end apart: 3, of which 2 were waited for; matrix products, arithmetic and copies ran while one was open for 1% of the time, Pallas kernels for 4%

profile of v3, /device:TPU:1, one launch (start us, length us, event | category | flops | bytes accessed | tf_op | source)
XLA Modules:
  0.0 138.3 jit_solution(3476661022522553462)
XLA Ops:
  0.6 0.0 copy-start.5
  0.6 0.0 copy-start.4
  0.7 0.0 copy-start.3
  0.7 0.0 copy-start.2
  0.7 0.0 copy-start.6
  0.7 0.8 copy-done.6
  1.4 0.0 copy-start.7
  1.4 0.7 copy-done.7
  2.1 0.0 copy-start.1
  2.1 0.0 copy-start.8
  2.1 0.9 spread.1
  3.0 10.4 %all-to-all-start = ((bf16[32,8,1024]{2,1,0:T(8,128)(2,1)}), bf16[32,8,1024]{2,1,0:T(8,128)(2,1)S(1)}, u32[]{:S(2)}, u32[]{:S(2)}) async-start(bf16[32,8,1024]{2,1,0:T(8,128)(2,1)} %spread.1), calls=%async_computation | async-start | bytes 1048576 | tf_op jit(solution)/shard_map/all_to_all | solution.py:230
  13.4 0.7 pad_add_fusion.slots
  14.1 0.0 copy-done.3
  14.1 0.0 copy-done.2
  14.1 0.0 copy-done.1
  14.1 2.1 %place.1 = (bf16[512,1024]{1,0:T(8,128)(2,1)S(1)}, bf16[512,1024]{1,0:T(8,128)(2,1)}, bf16[1024,512]{1,0:T(8,128)(2,1)}) custom-call(s32[3,10]{1,0:T(4,128)S(1)} %pad_add_fusion.slots, bf16[10,128,128]{2,1,0:T(8,128)(2,1)S(1)} %bitcast.16, bf16[10,128,128]{2,1,0:T(8,128)(2,1)S(1)} %bitcast.17, bf16[10,128,128]{2,1,0:T(8,128)(2,1)S(1)} %bitcast.18), custom_call_target="tpu_custom_call" | custom-call | tf_op jit(solution)/shard_map/place/pallas_call | solution.py:26
  16.2 8.9 %all-to-all-done = bf16[32,8,1024]{2,1,0:T(8,128)(2,1)S(1)} async-done(((bf16[32,8,1024]{2,1,0:T(8,128)(2,1)}), bf16[32,8,1024]{2,1,0:T(8,128)(2,1)S(1)}, u32[]{:S(2)}, u32[]{:S(2)}) %all-to-all-start) | async-done | bytes 524320 | tf_op jit(solution)/shard_map/all_to_all | solution.py:230
  25.1 0.0 copy-done.5
  25.1 0.0 copy-done.4
  25.1 0.0 copy-done.8
  25.1 3.3 %partials.1 = bf16[240,3456]{1,0:T(8,128)(2,1)S(1)} custom-call(bf16[256,1024]{1,0:T(8,128)(2,1)S(1)} %bitcast.14, bf16[512,1024]{1,0:T(8,128)(2,1)S(1)} %get-tuple-element.15.gate_w, bf16[240,256]{1,0:T(8,128)(2,1)S(1)} %copy-done.4, bf16[16,256]{1,0:T(8,128)(2,1)S(1)} %copy-done.8, bf16[240,128]{1,0:T(8,128)(2,1)S(1)} %copy-done.5, ...), custom_call_target="tpu_custom_call" | custom-call | tf_op jit(solution)/shard_map/partials/pallas_call | solution.py:26
  28.4 38.0 %fusion = bf16[16,3456]{1,0:T(8,128)(2,1)S(1)} fusion(bf16[240,3456]{1,0:T(8,128)(2,1)S(1)} %partials.1), kind=kCustom, calls=%all-reduce-scatter | all-reduce-scatter fusion | flops 884737 | bytes 1771520
  66.4 2.9 %collective-permute-start = (bf16[15,3456]{1,0:T(8,128)(2,1)S(1)}, bf16[15,3456]{1,0:T(8,128)(2,1)S(1)}, u32[]{:S(2)}, u32[]{:S(2)}) collective-permute-start(bf16[15,3456]{1,0:T(8,128)(2,1)S(1)} %slice), channel_id=1, source_target_pairs={{0,1},{1,2},{2,3},{3,4},{4,5},{5,6},{6,7},{7,8},{8,9},{9,10},{10,1... | collective-permute-start | bytes 311048
  69.3 1.3 dynamic-slice.4
  71.2 0.0 collective-permute-done
  71.3 0.3 concatenate
  71.6 0.2 hidden.1
  71.8 34.0 %all-gather.1 = f16[256,3200]{1,0:T(8,128)(2,1)S(1)} all-gather(f16[16,3200]{1,0:T(8,128)(2,1)S(1)} %convert_element_type.6), channel_id=1, replica_groups=mesh['row'=32,'col'=16] {'col'}, dimensions={0}, use_global_device_ids=true | all-gather | bytes 1740800 | tf_op jit(solution)/shard_map/all_gather | solution.py:254
  105.8 0.2 convert_element_type.7.gathered
  106.0 3.4 %outputs.1 = (bf16[256,3072]{1,0:T(8,128)(2,1)}, bf16[256,1024]{1,0:T(8,128)(2,1)}) custom-call(bf16[256,3200]{1,0:T(8,128)(2,1)S(1)} %convert_element_type.7.gathered, bf16[512,1024]{1,0:T(8,128)(2,1)S(1)} %get-tuple-element.15.gate_w, bf16[512,1024]{1,0:T(8,128)(2,1)} %get-tuple-element.16.up_far, bf16[1024,512]{1,0:T(8,128)(2,1)} %get-tuple-element.17.down_far), custom_call_target="tpu_custom_call" | custom-call | tf_op jit(solution)/shard_map/outputs/pallas_call | solution.py:26
  109.4 16.7 %all-to-all-start.1 = ((bf16[32,8,1024]{2,1,0:T(8,128)(2,1)}), bf16[32,8,1024]{2,1,0:T(8,128)(2,1)S(1)}, u32[]{:S(2)}, u32[]{:S(2)}) async-start(bf16[32,8,1024]{2,1,0:T(8,128)(2,1)} %bitcast.8), calls=%async_computation.1 | async-start | bytes 1048576 | tf_op jit(solution)/shard_map/all_to_all | solution.py:270
  126.1 0.0 copy-start
  126.1 1.4 %copy-done = bf16[256,3072]{1,0:T(8,128)(2,1)S(1)} copy-done((bf16[256,3072]{1,0:T(8,128)(2,1)S(1)}, bf16[256,3072]{1,0:T(8,128)(2,1)}, u32[]{:S(2)}) %copy-start) | copy-done | bytes 1572888
  127.5 4.1 %grads.3 = (f32[10,128,128]{2,1,0:T(8,128)}, f32[10,128,128]{2,1,0:T(8,128)}, f32[10,128,128]{2,1,0:T(8,128)}) custom-call(s32[3,10]{1,0:T(4,128)S(1)} %pad_add_fusion.slots, bf16[256,1024]{1,0:T(8,128)(2,1)S(1)} %bitcast.15, bf16[256,3072]{1,0:T(8,128)(2,1)S(1)} %copy-done), custom_call_target="tpu_custom_call" | custom-call | tf_op jit(solution)/shard_map/grads/pallas_call | solution.py:26
  131.6 6.1 %all-to-all-done.1.parts = bf16[32,8,1024]{2,1,0:T(8,128)(2,1)S(1)} async-done(((bf16[32,8,1024]{2,1,0:T(8,128)(2,1)}), bf16[32,8,1024]{2,1,0:T(8,128)(2,1)S(1)}, u32[]{:S(2)}, u32[]{:S(2)}) %all-to-all-start.1) | async-done | bytes 524320 | tf_op jit(solution)/shard_map/all_to_all | solution.py:270
  137.7 0.7 row_sum.1
  (3 shorter events, 0.1 us)
Async XLA Ops:
  0.6 24.5 %copy-start.5 = (bf16[240,128]{1,0:T(8,128)(2,1)S(1)}, bf16[240,128]{1,0:T(8,128)(2,1)}, u32[]{:S(2)}) copy-start(bf16[240,128]{1,0:T(8,128)(2,1)} %constant.8.clone.spot) | copy-start | bytes 184324
  0.6 24.5 %copy-start.4 = (bf16[240,256]{1,0:T(8,128)(2,1)S(1)}, bf16[240,256]{1,0:T(8,128)(2,1)}, u32[]{:S(2)}) copy-start(bf16[240,256]{1,0:T(8,128)(2,1)} %constant.6.clone.rows) | copy-start | bytes 368644
  0.7 13.4 %copy-start.3 = (bf16[1,1,10,128,128]{4,3,2,1,0:T(8,128)(2,1)S(1)}, bf16[1,1,10,128,128]{4,3,2,1,0:T(8,128)(2,1)}, u32[]{:S(2)}) copy-start(bf16[1,1,10,128,128]{4,3,2,1,0:T(8,128)(2,1)} %param.14) | copy-start | bytes 983044
  0.7 13.4 %copy-start.2 = (bf16[1,1,10,128,128]{4,3,2,1,0:T(8,128)(2,1)S(1)}, bf16[1,1,10,128,128]{4,3,2,1,0:T(8,128)(2,1)}, u32[]{:S(2)}) copy-start(bf16[1,1,10,128,128]{4,3,2,1,0:T(8,128)(2,1)} %param.13) | copy-start | bytes 983044
  0.7 0.8 copy-start.6
  1.4 0.7 copy-start.7
  2.1 12.0 %copy-start.1 = (bf16[1,1,10,128,128]{4,3,2,1,0:T(8,128)(2,1)S(1)}, bf16[1,1,10,128,128]{4,3,2,1,0:T(8,128)(2,1)}, u32[]{:S(2)}) copy-start(bf16[1,1,10,128,128]{4,3,2,1,0:T(8,128)(2,1)} %param.12) | copy-start | bytes 983044
  2.1 23.0 %copy-start.8 = (bf16[16,256]{1,0:T(8,128)(2,1)S(1)}, bf16[16,256]{1,0:T(8,128)(2,1)}, u32[]{:S(2)}) copy-start(bf16[16,256]{1,0:T(8,128)(2,1)} %constant.7.clone.last) | copy-start | bytes 24580
  3.0 22.1 %all-to-all-start = ((bf16[32,8,1024]{2,1,0:T(8,128)(2,1)}), bf16[32,8,1024]{2,1,0:T(8,128)(2,1)S(1)}, u32[]{:S(2)}, u32[]{:S(2)}) async-start(bf16[32,8,1024]{2,1,0:T(8,128)(2,1)} %spread.1), calls=%async_computation | async-start | bytes 1048576 | tf_op jit(solution)/shard_map/all_to_all | solution.py:230
  66.4 4.8 %collective-permute-start = (bf16[15,3456]{1,0:T(8,128)(2,1)S(1)}, bf16[15,3456]{1,0:T(8,128)(2,1)S(1)}, u32[]{:S(2)}, u32[]{:S(2)}) collective-permute-start(bf16[15,3456]{1,0:T(8,128)(2,1)S(1)} %slice), channel_id=1, source_target_pairs={{0,1},{1,2},{2,3},{3,4},{4,5},{5,6},{6,7},{7,8},{8,9},{9,10},{10,1... | collective-permute-start | bytes 311048
  109.4 28.3 %all-to-all-start.1 = ((bf16[32,8,1024]{2,1,0:T(8,128)(2,1)}), bf16[32,8,1024]{2,1,0:T(8,128)(2,1)S(1)}, u32[]{:S(2)}, u32[]{:S(2)}) async-start(bf16[32,8,1024]{2,1,0:T(8,128)(2,1)} %bitcast.8), calls=%async_computation.1 | async-start | bytes 1048576 | tf_op jit(solution)/shard_map/all_to_all | solution.py:270
  126.1 1.4 %copy-start = (bf16[256,3072]{1,0:T(8,128)(2,1)S(1)}, bf16[256,3072]{1,0:T(8,128)(2,1)}, u32[]{:S(2)}) copy-start(bf16[256,3072]{1,0:T(8,128)(2,1)} %get-tuple-element.21.hidden) | copy-start | bytes 4718596

commit v4 on v3

--- a/solution.py
+++ b/solution.py
@@ -1,6 +1,5 @@
 import jax
 import jax.numpy as jnp
-import numpy as np
 from jax import lax
 from jax.experimental import pallas as pl
 from jax.experimental.pallas import tpu as pltpu
@@ -9,7 +8,7 @@
 BLK = 128
 F32 = jnp.float32
 BF16 = jnp.bfloat16
-FLOOR = 2.0**-100
+GROUP = 64
 VMEM_BYTES = 20 * 2**20
 
 
@@ -81,21 +80,8 @@
     copies[2].wait()
 
 
-def row_moves(share, n_col):
-    keep = share - 1
-    rows = np.zeros((n_col * keep, n_col * share), np.float32)
-    last = np.zeros((n_col, n_col * share), np.float32)
-    spot = np.zeros((n_col * keep, 8 * n_col), np.float32)
-    for dev in range(n_col):
-        last[dev, dev * share + keep] = 1.0
-        for row in range(keep):
-            rows[dev * keep + row, dev * share + row] = 1.0
-        for blk in range(8):
-            spot[dev * keep + blk, blk * n_col + dev] = 1.0
-    return tuple(jnp.asarray(m, BF16) for m in (rows, last, spot))
-
-
-def partial_kernel(panel, gate_w, rows, last, spot, up_far, down_far, out, up_w, down_w, sems):
+def partial_kernel(panel, gate_w, up_far, down_far, *refs):
+    outs, (up_w, down_w, sems) = refs[:-3], refs[-3:]
     copies = {
         1: pltpu.make_async_copy(up_far, up_w, sems.at[0]),
         2: pltpu.make_async_copy(down_far, down_w, sems.at[1]),
@@ -103,58 +89,39 @@
     copies[1].start()
     copies[2].start()
     width, hid = gate_w.shape
-    main = dot(rows[...], panel[...], 1, 0).astype(BF16)
-    ends = dot(last[...], panel[...], 1, 0).astype(BF16)
+    blocks = hid // BLK
     jobs = ((0, gate_w, 0), (0, up_w, 0), (width, down_w, 1))
+    each = len(outs) // 3
     for which, (lo, weight, dim) in enumerate(jobs):
         if which > 0:
             copies[which].wait()
-        base = which * (hid + BLK)
-        tile = weight[...]
-        out[:, base : base + hid] = dot(main[:, lo : lo + width], tile, 1, dim).astype(BF16)
-        end = dot(ends[:, lo : lo + width], tile, 1, dim).astype(BF16)
-        pieces = [end[:, blk * BLK : (blk + 1) * BLK] for blk in range(hid // BLK)]
-        moved = dot(spot[...], jnp.concatenate(pieces, axis=0), 1, 0)
-        out[:, base + hid : base + hid + BLK] = moved.astype(BF16)
-
-
-def hidden_kernel(sums, out, full):
-    keep = sums.shape[0]
-    step = sums.shape[1] // 3
-    hid = step - BLK
-    gate, up, cot = (sums[:, i * step : (i + 1) * step].astype(F32) for i in range(3))
-    sig = jax.nn.sigmoid(gate)
-    act = gate * sig
-    results = (act * up, cot * up * (sig * (1.0 + gate * (1.0 - sig))), cot * act)
-    lane = lax.broadcasted_iota(jnp.int32, (keep + 1, BLK), 1)
-    powers = jnp.zeros((keep + 1, BLK), F32)
-    for which, value in enumerate(results):
-        value = value.astype(BF16).astype(F32)
-        full[0:keep, :] = value[:, :hid]
-        for blk in range(hid // BLK):
-            full[keep : keep + 1, blk * BLK : (blk + 1) * BLK] = value[blk : blk + 1, hid:]
-        value = full[...]
-        most = jnp.max(jnp.abs(value), axis=1, keepdims=True)
-        power = jnp.floor(jnp.log2(jnp.maximum(most, FLOOR)))
-        out[:, which * hid : (which + 1) * hid] = value * jnp.exp2(13.0 - power)
-        powers = jnp.where(lane == which, power, powers)
-    out[:, 3 * hid :] = powers
-
-
-def output_kernel(
-    gathered, gate_w, up_far, down_far, panel_out, out, panel, up_w, down_w, sems
-):
+        term = dot(panel[:, lo : lo + width], weight[...], 1, dim).astype(BF16)
+        for i in range(each):
+            row, col = (i // blocks) * GROUP, (i % blocks) * BLK
+            outs[which * each + i][...] = term[row : row + GROUP, col : col + BLK]
+
+
+def output_kernel(gate_w, up_far, down_far, *refs):
+    sums, (panel_out, out, panel, up_w, down_w, sems) = refs[:-6], refs[-6:]
     load_up = pltpu.make_async_copy(up_far, up_w, sems.at[0])
     load = pltpu.make_async_copy(down_far, down_w, sems.at[1])
     store = pltpu.make_async_copy(panel, panel_out, sems.at[2])
     load_up.start()
     load.start()
     width, hid = gate_w.shape
-    powers = gathered[:, 3 * hid :].astype(F32)
-    for which in range(3):
-        cols = slice(which * hid, (which + 1) * hid)
-        scale = jnp.exp2(powers[:, which : which + 1] - 13.0)
-        panel[:, cols] = (gathered[:, cols].astype(F32) * scale).astype(BF16)
+    blocks = hid // BLK
+    each = len(sums) // 3
+    for i in range(each):
+        gate, up, cot = (sums[k * each + i][...].astype(F32) for k in range(3))
+        sig = jax.nn.sigmoid(gate)
+        act = gate * sig
+        rows = slice((i // blocks) * GROUP, (i // blocks + 1) * GROUP)
+        col = (i % blocks) * BLK
+        panel[rows, col : col + BLK] = (act * up).astype(BF16)
+        panel[rows, hid + col : hid + col + BLK] = (
+            cot * up * (sig * (1.0 + gate * (1.0 - sig)))
+        ).astype(BF16)
+        panel[rows, 2 * hid + col : 2 * hid + col + BLK] = (cot * act).astype(BF16)
     store.start()
     load_up.wait()
     out[:, width:] = (
@@ -203,10 +170,9 @@
 def per_device(
     tokens, gate_blocks, up_blocks, down_blocks, gate_slots, up_slots, down_slots, out_grad
 ):
-    n_row, n_col = lax.axis_size("row"), lax.axis_size("col")
+    n_row = lax.axis_size("row")
     local, width = tokens.shape
     count = local * n_row
-    share = count // n_col
     hid = 8 * BLK
     wide = 3 * hid
     slots = jnp.stack([gate_slots[0, 0], up_slots[0, 0], down_slots[0, 0]])
@@ -229,33 +195,24 @@
     )
     panel = lax.all_to_all(spread, "row", 0, 0, tiled=True).reshape(count, 2 * width)
 
-    (terms,) = call(
+    terms = call(
         partial_kernel,
         (),
-        (panel, gate_w) + row_moves(share, n_col) + (up_w, down_w),
-        (((n_col * (share - 1), wide + 3 * BLK), BF16),),
+        (panel, gate_w, up_w, down_w),
+        (((GROUP, BLK), BF16),) * (3 * (count // GROUP) * (hid // BLK)),
         (
             pltpu.VMEM((width, hid), BF16),
             pltpu.VMEM((hid, width), BF16),
             pltpu.SemaphoreType.DMA((2,)),
         ),
         name="partials",
-        far=(5, 6),
-    )
-    sums = lax.psum_scatter(terms, "col", scatter_dimension=0, tiled=True)
-    (own,) = call(
-        hidden_kernel,
-        (),
-        (sums,),
-        (((share, wide + BLK), F32),),
-        (pltpu.VMEM((share, hid), F32),),
-        name="hidden",
-    )
-    gathered = lax.all_gather(own.astype(jnp.float16), "col", axis=0, tiled=True).astype(BF16)
+        far=(2, 3),
+    )
+    sums = lax.psum(tuple(terms), "col")
     hidden, out_terms = call(
         output_kernel,
         (),
-        (gathered, gate_w, up_w, down_w),
+        (gate_w, up_w, down_w) + tuple(sums),
         (((count, wide), BF16), ((count, 2 * width), BF16)),
         (
             pltpu.VMEM((count, wide), BF16),
@@ -264,7 +221,7 @@
             pltpu.SemaphoreType.DMA((3,)),
         ),
         name="outputs",
-        far=(2, 3),
+        far=(1, 2),
         far_outs=(0,),
     )
     parts = lax.all_to_all(

time: 139 us -> 163 us (1.17)
  local copies, waits for them, and re-layouts: 4.57 us -> 39.9 us
  blocking collectives: 72 us -> 64.1 us
  starting transfers between devices: 29.9 us -> 27.7 us
    psum x0 -> x1, blocking collectives: none -> 64.1 us  [per_device(): sums = lax.psum(tuple(terms), 'col')]
    unnamed x1 -> x0, blocking collectives: 38 us -> none
    unnamed x22 -> x162, local copies, waits for them, and re-layouts: 4.57 us -> 39.9 us
    all_gather x1 -> x0, blocking collectives: 34 us -> none  [per_device(): lax.all_gather(own.astype(jnp.float16), 'col', axis=0, tiled=True)]
    unnamed x1 -> x0, starting transfers between devices: 2.87 us -> none
    pallas_call x7 -> x6, Pallas kernels: 14.5 us -> 14.2 us  [call(): pl.pallas_call(kernel, out_shape=[pltpu.HBM(*out) if i in far_outs else j...]
  transfers between devices with their start and end apart: 3 -> 2, of which waited for: 2 -> 2; matrix products, arithmetic and copies ran while one was open for 1% -> 0% of each run, Pallas kernels for 4% -> 4%
where the time goes in v4:
time: 163 us; the launch traced here: 162 us
  blocking collectives  64.1 us (39%)
  local copies, waits for them, and re-layouts  39.9 us (24%)
  starting transfers between devices  27.7 us (17%)
  waiting for transfers between devices  15.1 us (9%)
  Pallas kernels  14.2 us (9%)
    psum x1, blocking collectives, per_device(): sums = lax.psum(tuple(terms), 'col')  64.1 us
    unnamed x162, local copies, waits for them, and re-layouts  39.9 us
    all_to_all x1, starting transfers between devices, per_device(): lax.all_to_all(out_terms.reshape(n_row, local, 2 * width), 'row', 0, 0, t...  17.3 us
    pallas_call x6, Pallas kernels, call(): pl.pallas_call(kernel, out_shape=[pltpu.HBM(*out) if i in far_outs else j...  14.2 us
    all_to_all x1, starting transfers between devices, per_device(): lax.all_to_all(spread, 'row', 0, 0, tiled=True).reshape(count, 2 * width)  10.4 us
    all_to_all x1, waiting for transfers between devices, per_device(): lax.all_to_all(spread, 'row', 0, 0, tiled=True).reshape(count, 2 * width)  9.51 us
    all_to_all x1, waiting for transfers between devices, per_device(): lax.all_to_all(out_terms.reshape(n_row, local, 2 * width), 'row', 0, 0, t...  5.64 us
  transfers between devices with their start and end apart: 2, of which 2 were waited for; matrix products, arithmetic and copies ran while one was open for 0% of the time, Pallas kernels for 4%

profile of v4, /device:TPU:1, one launch (start us, length us, event | category | flops | bytes accessed | tf_op | source)
XLA Modules:
  0.0 161.9 jit_solution(9208915977399131677)
XLA Ops:
  0.7 0.8 copy-done.76
  1.4 0.7 copy-done.77
  2.1 0.9 spread.1
  3.0 10.4 %all-to-all-start = ((bf16[32,8,1024]{2,1,0:T(8,128)(2,1)}), bf16[32,8,1024]{2,1,0:T(8,128)(2,1)S(1)}, u32[]{:S(2)}, u32[]{:S(2)}) async-start(bf16[32,8,1024]{2,1,0:T(8,128)(2,1)} %spread.1), calls=%async_computation | async-start | bytes 1048576 | tf_op jit(solution)/shard_map/all_to_all | solution.py:196
  13.4 2.1 %place.1 = (bf16[512,1024]{1,0:T(8,128)(2,1)S(1)}, bf16[512,1024]{1,0:T(8,128)(2,1)}, bf16[1024,512]{1,0:T(8,128)(2,1)}) custom-call(s32[3,10]{1,0:T(4,128)S(1)} %pad_add_fusion.slots, bf16[10,128,128]{2,1,0:T(8,128)(2,1)S(1)} %bitcast.13, bf16[10,128,128]{2,1,0:T(8,128)(2,1)S(1)} %bitcast.14, bf16[10,128,128]{2,1,0:T(8,128)(2,1)S(1)} %bitcast.15), custom_call_target="tpu_custom_call" | custom-call | tf_op jit(solution)/shard_map/place/pallas_call | solution.py:25
  15.6 9.5 %all-to-all-done = bf16[32,8,1024]{2,1,0:T(8,128)(2,1)S(1)} async-done(((bf16[32,8,1024]{2,1,0:T(8,128)(2,1)}), bf16[32,8,1024]{2,1,0:T(8,128)(2,1)S(1)}, u32[]{:S(2)}, u32[]{:S(2)}) %all-to-all-start) | async-done | bytes 524320 | tf_op jit(solution)/shard_map/all_to_all | solution.py:196
  25.1 2.6 %partials.1 = (bf16[64,128]{1,0:T(8,128)(2,1)S(1)}, bf16[64,128]{1,0:T(8,128)(2,1)S(1)}, bf16[64,128]{1,0:T(8,128)(2,1)S(1)}, bf16[64,128]{1,0:T(8,128)(2,1)S(1)...) custom-call(bf16[256,1024]{1,0:T(8,128)(2,1)S(1)} %bitcast.11, ...), custom_call_target="tpu_custom_call" | custom-call | tf_op jit(solution)/shard_map/partials/pallas_call | solution.py:25
  29.4 0.6 copy-done.18
  30.6 0.6 copy-done.20
  31.2 0.6 copy-done.21
  32.4 0.6 copy-done.23
  33.6 0.6 copy-done.25
  34.8 0.6 copy-done.27
  35.4 0.6 copy-done.28
  36.0 0.6 copy-done.29
  37.8 0.6 copy-done.32
  38.4 0.6 copy-done.33
  39.6 0.6 copy-done.35
  40.2 0.6 copy-done.36
  40.8 0.6 copy-done.37
  42.0 0.6 copy-done.39
  43.2 0.6 copy-done.41
  44.4 0.6 copy-done.43
  45.0 0.6 copy-done.44
  45.6 0.6 copy-done.45
  46.8 0.6 copy-done.47
  47.4 0.6 copy-done.48
  48.0 0.6 copy-done.49
  49.2 0.6 copy-done.51
  49.8 0.6 copy-done.52
  52.2 0.6 copy-done.56
  52.8 0.6 copy-done.57
  53.4 0.6 copy-done.58
  54.6 0.6 copy-done.60
  55.2 0.6 copy-done.61
  56.4 0.6 copy-done.63
  57.6 0.6 copy-done.65
  58.2 0.6 copy-done.66
  59.4 0.6 copy-done.68
  60.0 0.6 copy-done.69
  63.0 0.6 copy-done.74
  64.9 64.1 %all-reduce.2 = (bf16[64,128]{1,0:T(8,128)(2,1)S(1)}, bf16[64,128]{1,0:T(8,128)(2,1)S(1)}, bf16[64,128]{1,0:T(8,128)(2,1)S(1)}, bf16[64,128]{1,0:T(8,128)(2,1)S(...) all-reduce(bf16[64,128]{1,0:T(8,128)(2,1)S(1)} %get-tuple-element.1, ...), channel_id=1, replica_groups=mesh['row'=32,'col'=16] {'col'}, use_global_device_ids=true, to_apply=%region_0.0 | all-reduce | flops 786432 | bytes 3145728 | tf_op jit(solution)/shard_map/psum | solution.py:211
  129.0 3.4 %outputs.1 = (bf16[256,3072]{1,0:T(8,128)(2,1)}, bf16[256,1024]{1,0:T(8,128)(2,1)}) custom-call(bf16[512,1024]{1,0:T(8,128)(2,1)S(1)} %get-tuple-element.111.gate_w, bf16[512,1024]{1,0:T(8,128)(2,1)} %get-tuple-element.112.up_far, bf16[1024,512]{1,0:T(8,128)(2,1)} %get-tuple-element.113.down_far, bf16[64,128]{1,0:T(8,128)(2,1)S(1)} %get-tuple-element.217.refs_0_, ...), custom_call_target="tpu_custom_call" | custom-call | tf_op jit(solution)/shard_map/outputs/pallas_call | solution.py:25
  132.4 17.3 %all-to-all-start.1 = ((bf16[32,8,1024]{2,1,0:T(8,128)(2,1)}), bf16[32,8,1024]{2,1,0:T(8,128)(2,1)S(1)}, u32[]{:S(2)}, u32[]{:S(2)}) async-start(bf16[32,8,1024]{2,1,0:T(8,128)(2,1)} %bitcast.7), calls=%async_computation.1 | async-start | bytes 1048576 | tf_op jit(solution)/shard_map/all_to_all | solution.py:227
  149.7 1.4 copy-done
  151.1 4.5 %grads.3 = (f32[10,128,128]{2,1,0:T(8,128)}, f32[10,128,128]{2,1,0:T(8,128)}, f32[10,128,128]{2,1,0:T(8,128)}) custom-call(s32[3,10]{1,0:T(4,128)S(1)} %pad_add_fusion.slots, bf16[256,1024]{1,0:T(8,128)(2,1)S(1)} %bitcast.12, bf16[256,3072]{1,0:T(8,128)(2,1)S(1)} %copy-done), custom_call_target="tpu_custom_call" | custom-call | tf_op jit(solution)/shard_map/grads/pallas_call | solution.py:25
  155.6 5.6 %all-to-all-done.1.parts = bf16[32,8,1024]{2,1,0:T(8,128)(2,1)S(1)} async-done(((bf16[32,8,1024]{2,1,0:T(8,128)(2,1)}), bf16[32,8,1024]{2,1,0:T(8,128)(2,1)S(1)}, u32[]{:S(2)}, u32[]{:S(2)}) %all-to-all-start.1) | async-done | bytes 524320 | tf_op jit(solution)/shard_map/all_to_all | solution.py:227
  161.3 0.7 row_sum.1
  (126 shorter events, 16.7 us)
Async XLA Ops:
  0.6 12.8 %copy-start.3 = (bf16[1,1,10,128,128]{4,3,2,1,0:T(8,128)(2,1)S(1)}, bf16[1,1,10,128,128]{4,3,2,1,0:T(8,128)(2,1)}, u32[]{:S(2)}) copy-start(bf16[1,1,10,128,128]{4,3,2,1,0:T(8,128)(2,1)} %param.11) | copy-start | bytes 983044
  0.6 12.8 %copy-start.2 = (bf16[1,1,10,128,128]{4,3,2,1,0:T(8,128)(2,1)S(1)}, bf16[1,1,10,128,128]{4,3,2,1,0:T(8,128)(2,1)}, u32[]{:S(2)}) copy-start(bf16[1,1,10,128,128]{4,3,2,1,0:T(8,128)(2,1)} %param.10) | copy-start | bytes 983044
  0.7 0.8 copy-start.76
  1.4 0.7 copy-start.77
  2.1 11.3 %copy-start.78 = (s32[1,1,10]{2,1,0:T(1,128)S(1)}, s32[1,1,10]{2,1,0:T(1,128)}, u32[]{:S(2)}) copy-start(s32[1,1,10]{2,1,0:T(1,128)} %param.14) | copy-start | bytes 124
  2.1 11.3 %copy-start.79 = (s32[1,1,10]{2,1,0:T(1,128)S(1)}, s32[1,1,10]{2,1,0:T(1,128)}, u32[]{:S(2)}) copy-start(s32[1,1,10]{2,1,0:T(1,128)} %param.13) | copy-start | bytes 124
  2.1 11.3 %copy-start.80 = (s32[1,1,10]{2,1,0:T(1,128)S(1)}, s32[1,1,10]{2,1,0:T(1,128)}, u32[]{:S(2)}) copy-start(s32[1,1,10]{2,1,0:T(1,128)} %param.12) | copy-start | bytes 124
  2.1 11.3 %copy-start.1 = (bf16[1,1,10,128,128]{4,3,2,1,0:T(8,128)(2,1)S(1)}, bf16[1,1,10,128,128]{4,3,2,1,0:T(8,128)(2,1)}, u32[]{:S(2)}) copy-start(bf16[1,1,10,128,128]{4,3,2,1,0:T(8,128)(2,1)} %param.9) | copy-start | bytes 983044
  3.0 22.1 %all-to-all-start = ((bf16[32,8,1024]{2,1,0:T(8,128)(2,1)}), bf16[32,8,1024]{2,1,0:T(8,128)(2,1)S(1)}, u32[]{:S(2)}, u32[]{:S(2)}) async-start(bf16[32,8,1024]{2,1,0:T(8,128)(2,1)} %spread.1), calls=%async_computation | async-start | bytes 1048576 | tf_op jit(solution)/shard_map/all_to_all | solution.py:196
  29.4 0.6 copy-start.18
  30.6 0.6 copy-start.20
  31.2 0.6 copy-start.21
  32.4 0.6 copy-start.23
  34.8 0.6 copy-start.27
  35.4 0.6 copy-start.28
  36.0 0.6 copy-start.29
  37.8 0.6 copy-start.32
  38.4 0.6 copy-start.33
  39.6 0.6 copy-start.35
  40.8 0.6 copy-start.37
  42.0 0.6 copy-start.39
  44.4 0.6 copy-start.43
  45.0 0.6 copy-start.44
  45.6 0.6 copy-start.45
  46.8 0.6 copy-start.47
  47.4 0.6 copy-start.48
  48.0 0.6 copy-start.49
  52.8 0.6 copy-start.57
  53.4 0.6 copy-start.58
  54.6 0.6 copy-start.60
  55.2 0.6 copy-start.61
  56.4 0.6 copy-start.63
  57.6 0.6 copy-start.65
  58.2 0.6 copy-start.66
  63.0 0.6 copy-start.74
  64.2 0.6 copy-start.4
  64.2 0.6 copy-start.5
  64.2 0.6 copy-start.6
  64.2 0.6 copy-start.7
  64.2 0.6 copy-start.8
  64.2 0.6 copy-start.9
  64.2 0.6 copy-start.10
  64.2 0.6 copy-start.11
  64.2 0.6 copy-start.12
  64.2 0.6 copy-start.13
  64.2 0.6 copy-start.14
  132.4 28.9 %all-to-all-start.1 = ((bf16[32,8,1024]{2,1,0:T(8,128)(2,1)}), bf16[32,8,1024]{2,1,0:T(8,128)(2,1)S(1)}, u32[]{:S(2)}, u32[]{:S(2)}) async-start(bf16[32,8,1024]{2,1,0:T(8,128)(2,1)} %bitcast.7), calls=%async_computation.1 | async-start | bytes 1048576 | tf_op jit(solution)/shard_map/all_to_all | solution.py:227
  149.7 1.4 copy-start
  (35 other events, 20.9 us)

commit v5 on v4

--- a/solution.py
+++ b/solution.py
@@ -81,7 +81,7 @@
 
 
 def partial_kernel(panel, gate_w, up_far, down_far, *refs):
-    outs, (up_w, down_w, sems) = refs[:-3], refs[-3:]
+    outs, (up_w, down_w, blocks_v, sems, done) = refs[:-5], refs[-5:]
     copies = {
         1: pltpu.make_async_copy(up_far, up_w, sems.at[0]),
         2: pltpu.make_async_copy(down_far, down_w, sems.at[1]),
@@ -92,13 +92,24 @@
     blocks = hid // BLK
     jobs = ((0, gate_w, 0), (0, up_w, 0), (width, down_w, 1))
     each = len(outs) // 3
+    stores = []
     for which, (lo, weight, dim) in enumerate(jobs):
         if which > 0:
             copies[which].wait()
         term = dot(panel[:, lo : lo + width], weight[...], 1, dim).astype(BF16)
         for i in range(each):
             row, col = (i // blocks) * GROUP, (i % blocks) * BLK
-            outs[which * each + i][...] = term[row : row + GROUP, col : col + BLK]
+            blocks_v[which * each + i] = term[row : row + GROUP, col : col + BLK]
+            stores.append(
+                pltpu.make_async_copy(
+                    blocks_v.at[which * each + i],
+                    outs[which * each + i],
+                    done.at[which * each + i],
+                )
+            )
+            stores[-1].start()
+    for store in stores:
+        store.wait()
 
 
 def output_kernel(gate_w, up_far, down_far, *refs):
@@ -195,18 +206,22 @@
     )
     panel = lax.all_to_all(spread, "row", 0, 0, tiled=True).reshape(count, 2 * width)
 
+    n_blocks = 3 * (count // GROUP) * (hid // BLK)
     terms = call(
         partial_kernel,
         (),
         (panel, gate_w, up_w, down_w),
-        (((GROUP, BLK), BF16),) * (3 * (count // GROUP) * (hid // BLK)),
+        (((GROUP, BLK), BF16),) * n_blocks,
         (
             pltpu.VMEM((width, hid), BF16),
             pltpu.VMEM((hid, width), BF16),
+            pltpu.VMEM((n_blocks, GROUP, BLK), BF16),
             pltpu.SemaphoreType.DMA((2,)),
+            pltpu.SemaphoreType.DMA((n_blocks,)),
         ),
         name="partials",
         far=(2, 3),
+        far_outs=tuple(range(n_blocks)),
     )
     sums = lax.psum(tuple(terms), "col")
     hidden, out_terms = call(

time: 163 us -> 127 us (0.78)
  local copies, waits for them, and re-layouts: 39.9 us -> 2.87 us
    unnamed x162 -> x18, local copies, waits for them, and re-layouts: 39.9 us -> 2.87 us
  transfers between devices with their start and end apart: 2 -> 2, of which waited for: 2 -> 2; matrix products, arithmetic and copies ran while one was open for 0% -> 0% of each run, Pallas kernels for 4% -> 5%
where the time goes in v5:
time: 127 us
  blocking collectives  64.1 us (50%)
  starting transfers between devices  27.7 us (22%)
  waiting for transfers between devices  15.9 us (13%)
  Pallas kernels  15.2 us (12%)
  local copies, waits for them, and re-layouts  2.87 us (2%)
    psum x1, blocking collectives, per_device(): sums = lax.psum(tuple(terms), 'col')  64.1 us
    all_to_all x1, starting transfers between devices, per_device(): lax.all_to_all(out_terms.reshape(n_row, local, 2 * width), 'row', 0, 0, t...  17.3 us
    pallas_call x6, Pallas kernels, call(): pl.pallas_call(kernel, out_shape=[pltpu.HBM(*out) if i in far_outs else j...  15.2 us
    all_to_all x1, starting transfers between devices, per_device(): lax.all_to_all(spread, 'row', 0, 0, tiled=True).reshape(count, 2 * width)  10.4 us
    all_to_all x1, waiting for transfers between devices, per_device(): lax.all_to_all(spread, 'row', 0, 0, tiled=True).reshape(count, 2 * width)  9.55 us
    all_to_all x1, waiting for transfers between devices, per_device(): lax.all_to_all(out_terms.reshape(n_row, local, 2 * width), 'row', 0, 0, t...  6.37 us
    unnamed x18, local copies, waits for them, and re-layouts  2.87 us
  transfers between devices with their start and end apart: 2, of which 2 were waited for; matrix products, arithmetic and copies ran while one was open for 0% of the time, Pallas kernels for 5%

profile of v5, /device:TPU:1, one launch (start us, length us, event | category | flops | bytes accessed | tf_op | source)
XLA Modules:
  0.0 126.5 jit_solution(6470071647542566702)
XLA Ops:
  0.6 0.0 copy-start.3
  0.6 0.0 copy-start.2
  0.7 0.0 copy-start.4
  0.7 0.8 copy-done.4
  1.4 0.0 copy-start.5
  1.4 0.7 copy-done.5
  2.1 0.0 copy-start.6
  2.1 0.0 copy-start.7
  2.1 0.0 copy-start.8
  2.1 0.0 copy-start.1
  2.1 0.9 spread.1
  3.0 10.4 %all-to-all-start = ((bf16[32,8,1024]{2,1,0:T(8,128)(2,1)}), bf16[32,8,1024]{2,1,0:T(8,128)(2,1)S(1)}, u32[]{:S(2)}, u32[]{:S(2)}) async-start(bf16[32,8,1024]{2,1,0:T(8,128)(2,1)} %spread.1), calls=%async_computation | async-start | bytes 1048576 | tf_op jit(solution)/shard_map/all_to_all | solution.py:207
  13.4 0.0 copy-done.6
  13.4 0.0 copy-done.7
  13.4 0.0 copy-done.8
  13.4 0.0 copy-done.3
  13.4 0.0 copy-done.2
  13.4 0.0 copy-done.1
  13.4 2.1 %place.1 = (bf16[512,1024]{1,0:T(8,128)(2,1)S(1)}, bf16[512,1024]{1,0:T(8,128)(2,1)}, bf16[1024,512]{1,0:T(8,128)(2,1)}) custom-call(s32[3,10]{1,0:T(4,128)S(1)} %pad_add_fusion.slots, bf16[10,128,128]{2,1,0:T(8,128)(2,1)S(1)} %bitcast.13, bf16[10,128,128]{2,1,0:T(8,128)(2,1)S(1)} %bitcast.14, bf16[10,128,128]{2,1,0:T(8,128)(2,1)S(1)} %bitcast.15), custom_call_target="tpu_custom_call" | custom-call | tf_op jit(solution)/shard_map/place/pallas_call | solution.py:25
  15.5 9.6 %all-to-all-done = bf16[32,8,1024]{2,1,0:T(8,128)(2,1)S(1)} async-done(((bf16[32,8,1024]{2,1,0:T(8,128)(2,1)}), bf16[32,8,1024]{2,1,0:T(8,128)(2,1)S(1)}, u32[]{:S(2)}, u32[]{:S(2)}) %all-to-all-start) | async-done | bytes 524320 | tf_op jit(solution)/shard_map/all_to_all | solution.py:207
  25.1 4.3 %partials.1 = (bf16[64,128]{1,0:T(8,128)(2,1)}, bf16[64,128]{1,0:T(8,128)(2,1)}, bf16[64,128]{1,0:T(8,128)(2,1)}, bf16[64,128]{1,0:T(8,128)(2,1)}, bf16[64,128]{...) custom-call(bf16[256,1024]{1,0:T(8,128)(2,1)S(1)} %bitcast.11, ...), custom_call_target="tpu_custom_call" | custom-call | tf_op jit(solution)/shard_map/partials/pallas_call | solution.py:25
  29.4 64.1 %all-reduce.2 = (bf16[64,128]{1,0:T(8,128)(2,1)S(1)}, bf16[64,128]{1,0:T(8,128)(2,1)S(1)}, bf16[64,128]{1,0:T(8,128)(2,1)S(1)}, bf16[64,128]{1,0:T(8,128)(2,1)S(...) all-reduce(bf16[64,128]{1,0:T(8,128)(2,1)} %get-tuple-element.114, ...), channel_id=1, replica_groups=mesh['row'=32,'col'=16] {'col'}, use_global_device_ids=true, to_apply=%region_0.0 | all-reduce | flops 786432 | bytes 3145728 | tf_op jit(solution)/shard_map/psum | solution.py:226
  93.5 3.4 %outputs.1 = (bf16[256,3072]{1,0:T(8,128)(2,1)}, bf16[256,1024]{1,0:T(8,128)(2,1)}) custom-call(bf16[512,1024]{1,0:T(8,128)(2,1)S(1)} %get-tuple-element.111.gate_w, bf16[512,1024]{1,0:T(8,128)(2,1)} %get-tuple-element.112.up_far, bf16[1024,512]{1,0:T(8,128)(2,1)} %get-tuple-element.113.down_far, bf16[64,128]{1,0:T(8,128)(2,1)S(1)} %get-tuple-element.217.refs_0_, ...), custom_call_target="tpu_custom_call" | custom-call | tf_op jit(solution)/shard_map/outputs/pallas_call | solution.py:25
  97.0 17.3 %all-to-all-start.1 = ((bf16[32,8,1024]{2,1,0:T(8,128)(2,1)}), bf16[32,8,1024]{2,1,0:T(8,128)(2,1)S(1)}, u32[]{:S(2)}, u32[]{:S(2)}) async-start(bf16[32,8,1024]{2,1,0:T(8,128)(2,1)} %bitcast.7), calls=%async_computation.1 | async-start | bytes 1048576 | tf_op jit(solution)/shard_map/all_to_all | solution.py:242
  114.2 0.0 copy-start
  114.2 1.4 %copy-done = bf16[256,3072]{1,0:T(8,128)(2,1)S(1)} copy-done((bf16[256,3072]{1,0:T(8,128)(2,1)S(1)}, bf16[256,3072]{1,0:T(8,128)(2,1)}, u32[]{:S(2)}) %copy-start) | copy-done | bytes 1572888
  115.6 3.8 %grads.3 = (f32[10,128,128]{2,1,0:T(8,128)}, f32[10,128,128]{2,1,0:T(8,128)}, f32[10,128,128]{2,1,0:T(8,128)}) custom-call(s32[3,10]{1,0:T(4,128)S(1)} %pad_add_fusion.slots, bf16[256,1024]{1,0:T(8,128)(2,1)S(1)} %bitcast.12, bf16[256,3072]{1,0:T(8,128)(2,1)S(1)} %copy-done), custom_call_target="tpu_custom_call" | custom-call | tf_op jit(solution)/shard_map/grads/pallas_call | solution.py:25
  119.5 6.4 %all-to-all-done.1.parts = bf16[32,8,1024]{2,1,0:T(8,128)(2,1)S(1)} async-done(((bf16[32,8,1024]{2,1,0:T(8,128)(2,1)}), bf16[32,8,1024]{2,1,0:T(8,128)(2,1)S(1)}, u32[]{:S(2)}, u32[]{:S(2)}) %all-to-all-start.1) | async-done | bytes 524320 | tf_op jit(solution)/shard_map/all_to_all | solution.py:242
  125.8 0.7 row_sum.1
  (1 shorter events, 0.0 us)
Async XLA Ops:
  0.6 12.8 %copy-start.3 = (bf16[1,1,10,128,128]{4,3,2,1,0:T(8,128)(2,1)S(1)}, bf16[1,1,10,128,128]{4,3,2,1,0:T(8,128)(2,1)}, u32[]{:S(2)}) copy-start(bf16[1,1,10,128,128]{4,3,2,1,0:T(8,128)(2,1)} %param.11) | copy-start | bytes 983044
  0.6 12.8 %copy-start.2 = (bf16[1,1,10,128,128]{4,3,2,1,0:T(8,128)(2,1)S(1)}, bf16[1,1,10,128,128]{4,3,2,1,0:T(8,128)(2,1)}, u32[]{:S(2)}) copy-start(bf16[1,1,10,128,128]{4,3,2,1,0:T(8,128)(2,1)} %param.10) | copy-start | bytes 983044
  0.7 0.8 copy-start.4
  1.4 0.7 copy-start.5
  2.1 11.3 %copy-start.6 = (s32[1,1,10]{2,1,0:T(1,128)S(1)}, s32[1,1,10]{2,1,0:T(1,128)}, u32[]{:S(2)}) copy-start(s32[1,1,10]{2,1,0:T(1,128)} %param.14) | copy-start | bytes 124
  2.1 11.3 %copy-start.7 = (s32[1,1,10]{2,1,0:T(1,128)S(1)}, s32[1,1,10]{2,1,0:T(1,128)}, u32[]{:S(2)}) copy-start(s32[1,1,10]{2,1,0:T(1,128)} %param.13) | copy-start | bytes 124
  2.1 11.3 %copy-start.8 = (s32[1,1,10]{2,1,0:T(1,128)S(1)}, s32[1,1,10]{2,1,0:T(1,128)}, u32[]{:S(2)}) copy-start(s32[1,1,10]{2,1,0:T(1,128)} %param.12) | copy-start | bytes 124
  2.1 11.3 %copy-start.1 = (bf16[1,1,10,128,128]{4,3,2,1,0:T(8,128)(2,1)S(1)}, bf16[1,1,10,128,128]{4,3,2,1,0:T(8,128)(2,1)}, u32[]{:S(2)}) copy-start(bf16[1,1,10,128,128]{4,3,2,1,0:T(8,128)(2,1)} %param.9) | copy-start | bytes 983044
  3.0 22.1 %all-to-all-start = ((bf16[32,8,1024]{2,1,0:T(8,128)(2,1)}), bf16[32,8,1024]{2,1,0:T(8,128)(2,1)S(1)}, u32[]{:S(2)}, u32[]{:S(2)}) async-start(bf16[32,8,1024]{2,1,0:T(8,128)(2,1)} %spread.1), calls=%async_computation | async-start | bytes 1048576 | tf_op jit(solution)/shard_map/all_to_all | solution.py:207
  97.0 28.9 %all-to-all-start.1 = ((bf16[32,8,1024]{2,1,0:T(8,128)(2,1)}), bf16[32,8,1024]{2,1,0:T(8,128)(2,1)S(1)}, u32[]{:S(2)}, u32[]{:S(2)}) async-start(bf16[32,8,1024]{2,1,0:T(8,128)(2,1)} %bitcast.7), calls=%async_computation.1 | async-start | bytes 1048576 | tf_op jit(solution)/shard_map/all_to_all | solution.py:242
  114.2 1.4 %copy-start = (bf16[256,3072]{1,0:T(8,128)(2,1)S(1)}, bf16[256,3072]{1,0:T(8,128)(2,1)}, u32[]{:S(2)}) copy-start(bf16[256,3072]{1,0:T(8,128)(2,1)} %get-tuple-element.213.hidden) | copy-start | bytes 4718596

commit v6 on v5

--- a/solution.py
+++ b/solution.py
@@ -9,6 +9,7 @@
 F32 = jnp.float32
 BF16 = jnp.bfloat16
 GROUP = 64
+CHUNK = 256
 VMEM_BYTES = 20 * 2**20
 
 
@@ -49,97 +50,120 @@
     )
 
 
-def spread_kernel(tokens, grads, out):
+def spread_kernel(tokens, grads, out, sems):
     width = tokens.shape[1]
-    out[:, :, :width] = jnp.broadcast_to(tokens[...][None], (out.shape[0],) + tokens.shape)
-    out[:, :, width:] = jnp.broadcast_to(grads[...][None], (out.shape[0],) + grads.shape)
+    copies = []
+    for row in range(out.shape[0]):
+        for half, source in enumerate((tokens, grads)):
+            copies.append(
+                pltpu.make_async_copy(
+                    source,
+                    out.at[row, :, half * width : (half + 1) * width],
+                    sems.at[row, half],
+                )
+            )
+            copies[-1].start()
+    for copy in copies:
+        copy.wait()
 
 
 def place_kernel(
-    slots, gate_blk, up_blk, down_blk, gate_ref, up_out, down_out, up_ref, down_ref, sems
+    slots, gate_blk, up_blk, down_blk, gate_ref, up_out, down_t_out, gate_t_out, up_t_out, down_out,
+    up_ref, down_t, gate_t, up_t, down_ref, sems,
 ):
-    tiles = ((down_blk, down_ref, 2), (up_blk, up_ref, 1), (gate_blk, gate_ref, 0))
-    copies = {
-        1: pltpu.make_async_copy(up_ref, up_out, sems.at[0]),
-        2: pltpu.make_async_copy(down_ref, down_out, sems.at[1]),
-    }
-    for blk, ref, which in tiles:
+    jobs = (
+        (2, down_blk, down_t, True, down_t_out, 4),
+        (1, up_blk, up_ref, False, up_out, 8),
+        (0, gate_blk, gate_ref, False, None, 8),
+        (0, gate_blk, gate_t, True, gate_t_out, 8),
+        (1, up_blk, up_t, True, up_t_out, 8),
+        (2, down_blk, down_ref, False, down_out, 4),
+    )
+    copies = []
+    for job, (which, blk, ref, flip, out, col_blocks) in enumerate(jobs):
         ref[...] = jnp.zeros_like(ref)
-        col_blocks = ref.shape[1] // BLK
-        total = (ref.shape[0] // BLK) * col_blocks
+        total = (ref.shape[0] // BLK) * (ref.shape[1] // BLK)
         for slot in range(blk.shape[0]):
             number = slots[which, slot]
 
             @pl.when(number < total)
-            def _(number=number, slot=slot, blk=blk, ref=ref, col_blocks=col_blocks):
-                ref[at(number // col_blocks, BLK), at(number % col_blocks, BLK)] = blk[slot]
-
-        if which > 0:
-            copies[which].start()
-    copies[1].wait()
-    copies[2].wait()
+            def _(number=number, slot=slot, blk=blk, ref=ref, flip=flip, n=col_blocks):
+                row, col = number // n, number % n
+                if flip:
+                    ref[at(col, BLK), at(row, BLK)] = blk[slot].T
+                else:
+                    ref[at(row, BLK), at(col, BLK)] = blk[slot]
+
+        if out is not None:
+            copies.append(pltpu.make_async_copy(ref, out, sems.at[job]))
+            copies[-1].start()
+    for copy in copies:
+        copy.wait()
 
 
 def partial_kernel(panel, gate_w, up_far, down_far, *refs):
-    outs, (up_w, down_w, blocks_v, sems, done) = refs[:-5], refs[-5:]
+    outs, (up_w, down_t, blocks_v, sems, done) = refs[:-5], refs[-5:]
     copies = {
         1: pltpu.make_async_copy(up_far, up_w, sems.at[0]),
-        2: pltpu.make_async_copy(down_far, down_w, sems.at[1]),
+        2: pltpu.make_async_copy(down_far, down_t, sems.at[1]),
     }
     copies[1].start()
     copies[2].start()
     width, hid = gate_w.shape
-    blocks = hid // BLK
-    jobs = ((0, gate_w, 0), (0, up_w, 0), (width, down_w, 1))
-    each = len(outs) // 3
+    groups = panel.shape[0] // GROUP
     stores = []
-    for which, (lo, weight, dim) in enumerate(jobs):
+    for which, (lo, weight) in enumerate(((0, gate_w), (0, up_w), (width, down_t))):
         if which > 0:
             copies[which].wait()
-        term = dot(panel[:, lo : lo + width], weight[...], 1, dim).astype(BF16)
-        for i in range(each):
-            row, col = (i // blocks) * GROUP, (i % blocks) * BLK
-            blocks_v[which * each + i] = term[row : row + GROUP, col : col + BLK]
-            stores.append(
-                pltpu.make_async_copy(
-                    blocks_v.at[which * each + i],
-                    outs[which * each + i],
-                    done.at[which * each + i],
-                )
-            )
-            stores[-1].start()
+        for chunk in range(hid // CHUNK):
+            cols = slice(chunk * CHUNK, (chunk + 1) * CHUNK)
+            term = dot(panel[:, lo : lo + width], weight[:, cols], 1, 0).astype(BF16)
+            for row in range(groups):
+                for col in range(CHUNK // BLK):
+                    i = len(stores)
+                    blocks_v[i] = term[
+                        row * GROUP : (row + 1) * GROUP, col * BLK : (col + 1) * BLK
+                    ]
+                    stores.append(pltpu.make_async_copy(blocks_v.at[i], outs[i], done.at[i]))
+                    stores[-1].start()
     for store in stores:
         store.wait()
 
 
-def output_kernel(gate_w, up_far, down_far, *refs):
-    sums, (panel_out, out, panel, up_w, down_w, sems) = refs[:-6], refs[-6:]
-    load_up = pltpu.make_async_copy(up_far, up_w, sems.at[0])
-    load = pltpu.make_async_copy(down_far, down_w, sems.at[1])
-    store = pltpu.make_async_copy(panel, panel_out, sems.at[2])
-    load_up.start()
-    load.start()
-    width, hid = gate_w.shape
-    blocks = hid // BLK
+def output_kernel(gate_far, up_far, down_far, *refs):
+    sums, (panel_out, out, panel, gate_t, up_t, down_w, sems) = refs[:-7], refs[-7:]
+    loads = [
+        pltpu.make_async_copy(far, near, sems.at[i])
+        for i, (far, near) in enumerate(((gate_far, gate_t), (up_far, up_t), (down_far, down_w)))
+    ]
+    store = pltpu.make_async_copy(panel, panel_out, sems.at[3])
+    for load in loads:
+        load.start()
+    hid, width = gate_t.shape
+    groups = panel.shape[0] // GROUP
     each = len(sums) // 3
-    for i in range(each):
-        gate, up, cot = (sums[k * each + i][...].astype(F32) for k in range(3))
-        sig = jax.nn.sigmoid(gate)
-        act = gate * sig
-        rows = slice((i // blocks) * GROUP, (i // blocks + 1) * GROUP)
-        col = (i % blocks) * BLK
-        panel[rows, col : col + BLK] = (act * up).astype(BF16)
-        panel[rows, hid + col : hid + col + BLK] = (
-            cot * up * (sig * (1.0 + gate * (1.0 - sig)))
-        ).astype(BF16)
-        panel[rows, 2 * hid + col : 2 * hid + col + BLK] = (cot * act).astype(BF16)
+    i = 0
+    for chunk in range(hid // CHUNK):
+        for row in range(groups):
+            for blk in range(CHUNK // BLK):
+                gate, up, cot = (sums[k * each + i][...].astype(F32) for k in range(3))
+                i += 1
+                sig = jax.nn.sigmoid(gate)
+                act = gate * sig
+                rows = slice(row * GROUP, (row + 1) * GROUP)
+                col = chunk * CHUNK + blk * BLK
+                panel[rows, col : col + BLK] = (act * up).astype(BF16)
+                panel[rows, hid + col : hid + col + BLK] = (
+                    cot * up * (sig * (1.0 + gate * (1.0 - sig)))
+                ).astype(BF16)
+                panel[rows, 2 * hid + col : 2 * hid + col + BLK] = (cot * act).astype(BF16)
     store.start()
-    load_up.wait()
+    for load in loads:
+        load.wait()
     out[:, width:] = (
-        dot(panel[:, hid : 2 * hid], gate_w[...], 1, 1)
-        + dot(panel[:, 2 * hid :], up_w[...], 1, 1)
+        dot(panel[:, hid : 2 * hid], gate_t[...], 1, 0)
+        + dot(panel[:, 2 * hid :], up_t[...], 1, 0)
     ).astype(BF16)
-    load.wait()
     out[:, :width] = dot(panel[:, :hid], down_w[...], 1, 0).astype(BF16)
     store.wait()
 
@@ -188,21 +212,31 @@
     wide = 3 * hid
     slots = jnp.stack([gate_slots[0, 0], up_slots[0, 0], down_slots[0, 0]])
 
-    gate_w, up_w, down_w = call(
+    gate_w, up_w, down_t, gate_t, up_t, down_w = call(
         place_kernel,
         (slots,),
         (gate_blocks[0, 0], up_blocks[0, 0], down_blocks[0, 0]),
-        (((width, hid), BF16), ((width, hid), BF16), ((hid, width), BF16)),
+        tuple((shape, BF16) for shape in ((width, hid),) * 3 + ((hid, width),) * 3),
         (
             pltpu.VMEM((width, hid), BF16),
-            pltpu.VMEM((hid, width), BF16),
-            pltpu.SemaphoreType.DMA((2,)),
+            pltpu.VMEM((width, hid), BF16),
+            pltpu.VMEM((hid, width), BF16),
+            pltpu.VMEM((hid, width), BF16),
+            pltpu.VMEM((hid, width), BF16),
+            pltpu.SemaphoreType.DMA((6,)),
         ),
         name="place",
-        far_outs=(1, 2),
+        far_outs=(1, 2, 3, 4, 5),
     )
     (spread,) = call(
-        spread_kernel, (), (tokens, out_grad), (((n_row, local, 2 * width), BF16),), name="spread"
+        spread_kernel,
+        (),
+        (tokens, out_grad),
+        (((n_row, local, 2 * width), BF16),),
+        (pltpu.SemaphoreType.DMA((n_row, 2)),),
+        name="spread",
+        far=(0, 1),
+        far_outs=(0,),
     )
     panel = lax.all_to_all(spread, "row", 0, 0, tiled=True).reshape(count, 2 * width)
 
@@ -210,11 +244,11 @@
     terms = call(
         partial_kernel,
         (),
-        (panel, gate_w, up_w, down_w),
+        (panel, gate_w, up_w, down_t),
         (((GROUP, BLK), BF16),) * n_blocks,
         (
             pltpu.VMEM((width, hid), BF16),
-            pltpu.VMEM((hid, width), BF16),
+            pltpu.VMEM((width, hid), BF16),
             pltpu.VMEM((n_blocks, GROUP, BLK), BF16),
             pltpu.SemaphoreType.DMA((2,)),
             pltpu.SemaphoreType.DMA((n_blocks,)),
@@ -227,16 +261,17 @@
     hidden, out_terms = call(
         output_kernel,
         (),
-        (gate_w, up_w, down_w) + tuple(sums),
+        (gate_t, up_t, down_w) + tuple(sums),
         (((count, wide), BF16), ((count, 2 * width), BF16)),
         (
             pltpu.VMEM((count, wide), BF16),
-            pltpu.VMEM((width, hid), BF16),
-            pltpu.VMEM((hid, width), BF16),
-            pltpu.SemaphoreType.DMA((3,)),
+            pltpu.VMEM((hid, width), BF16),
+            pltpu.VMEM((hid, width), BF16),
+            pltpu.VMEM((hid, width), BF16),
+            pltpu.SemaphoreType.DMA((4,)),
         ),
         name="outputs",
-        far=(1, 2),
+        far=(0, 1, 2),
         far_outs=(0,),
     )
     parts = lax.all_to_all(

time: 127 us -> 143 us (1.13)
  Pallas kernels: 15.2 us -> 34 us
  local copies, waits for them, and re-layouts: 2.87 us -> 1.43 us
    pallas_call x6, Pallas kernels: 15.2 us -> 34 us  [call(): pl.pallas_call(kernel, out_shape=[pltpu.HBM(*out) if i in far_outs else j...]
    unnamed x18 -> x14, local copies, waits for them, and re-layouts: 2.87 us -> 1.43 us
where the time goes in v6:
time: 143 us
  blocking collectives  64.1 us (45%)
  Pallas kernels  34 us (24%)
  starting transfers between devices  27.7 us (19%)
  waiting for transfers between devices  14.6 us (10%)
  local copies, waits for them, and re-layouts  1.43 us (1%)
    psum x1, blocking collectives, per_device(): sums = lax.psum(tuple(terms), 'col')  64.1 us
    pallas_call x6, Pallas kernels, call(): pl.pallas_call(kernel, out_shape=[pltpu.HBM(*out) if i in far_outs else j...  34 us
    all_to_all x1, starting transfers between devices, per_device(): lax.all_to_all(out_terms.reshape(n_row, local, 2 * width), 'row', 0, 0, t...  17.3 us
    all_to_all x1, starting transfers between devices, per_device(): lax.all_to_all(spread, 'row', 0, 0, tiled=True).reshape(count, 2 * width)  10.4 us
    all_to_all x1, waiting for transfers between devices, per_device(): lax.all_to_all(spread, 'row', 0, 0, tiled=True).reshape(count, 2 * width)  8.4 us
    all_to_all x1, waiting for transfers between devices, per_device(): lax.all_to_all(out_terms.reshape(n_row, local, 2 * width), 'row', 0, 0, t...  6.22 us
  transfers between devices with their start and end apart: 2, of which 2 were waited for; matrix products, arithmetic and copies ran while one was open for 0% of the time, Pallas kernels for 5%

profile of v6, /device:TPU:1, one launch (start us, length us, event | category | flops | bytes accessed | tf_op | source)
XLA Modules:
  0.0 142.6 jit_solution(9359111573905071358)
XLA Ops:
  0.6 0.0 copy-start.4
  0.6 0.0 copy-start.5
  0.7 0.0 copy-start.6
  0.7 0.0 copy-start.3
  0.7 0.0 copy-start.2
  0.7 0.0 copy-start.1
  0.7 17.6 %spread.1 = bf16[32,8,1024]{2,1,0:T(8,128)(2,1)} custom-call(bf16[8,512]{1,0:T(8,128)(2,1)} %tokens.1, bf16[8,512]{1,0:T(8,128)(2,1)} %grads.2), custom_call_target="tpu_custom_call" | custom-call | tf_op jit(solution)/shard_map/spread/pallas_call | solution.py:26
  18.3 10.4 %all-to-all-start = ((bf16[32,8,1024]{2,1,0:T(8,128)(2,1)}), bf16[32,8,1024]{2,1,0:T(8,128)(2,1)S(1)}, u32[]{:S(2)}, u32[]{:S(2)}) async-start(bf16[32,8,1024]{2,1,0:T(8,128)(2,1)} %spread.1), calls=%async_computation | async-start | bytes 1048576 | tf_op jit(solution)/shard_map/all_to_all | solution.py:241
  28.7 0.0 copy-done.4
  28.7 0.0 copy-done.5
  28.7 0.0 copy-done.6
  28.7 0.0 copy-done.3
  28.7 0.0 copy-done.2
  28.7 0.0 copy-done.1
  28.8 3.2 %place.1 = (bf16[512,1024]{1,0:T(8,128)(2,1)S(1)}, bf16[512,1024]{1,0:T(8,128)(2,1)}, bf16[512,1024]{1,0:T(8,128)(2,1)}, bf16[1024,512]{1,0:T(8,128)(2,1)}, bf16...) custom-call(s32[3,10]{1,0:T(4,128)S(1)} %pad_add_fusion.slots, bf16[10,128,128]{2,1,0:T(8,128)(2,1)S(1)} %bitcast.13, ...), custom_call_target="tpu_custom_call" | custom-call | tf_op jit(solution)/shard_map/place/pallas_call | solution.py:26
  32.0 8.4 %all-to-all-done = bf16[32,8,1024]{2,1,0:T(8,128)(2,1)S(1)} async-done(((bf16[32,8,1024]{2,1,0:T(8,128)(2,1)}), bf16[32,8,1024]{2,1,0:T(8,128)(2,1)S(1)}, u32[]{:S(2)}, u32[]{:S(2)}) %all-to-all-start) | async-done | bytes 524320 | tf_op jit(solution)/shard_map/all_to_all | solution.py:241
  40.4 4.2 %partials.1 = (bf16[64,128]{1,0:T(8,128)(2,1)}, bf16[64,128]{1,0:T(8,128)(2,1)}, bf16[64,128]{1,0:T(8,128)(2,1)}, bf16[64,128]{1,0:T(8,128)(2,1)}, bf16[64,128]{...) custom-call(bf16[256,1024]{1,0:T(8,128)(2,1)S(1)} %bitcast.11, ...), custom_call_target="tpu_custom_call" | custom-call | tf_op jit(solution)/shard_map/partials/pallas_call | solution.py:26
  44.6 64.1 %all-reduce.2 = (bf16[64,128]{1,0:T(8,128)(2,1)S(1)}, bf16[64,128]{1,0:T(8,128)(2,1)S(1)}, bf16[64,128]{1,0:T(8,128)(2,1)S(1)}, bf16[64,128]{1,0:T(8,128)(2,1)S(...) all-reduce(bf16[64,128]{1,0:T(8,128)(2,1)} %get-tuple-element.120, ...), channel_id=1, replica_groups=mesh['row'=32,'col'=16] {'col'}, use_global_device_ids=true, to_apply=%region_0.0 | all-reduce | flops 786432 | bytes 3145728 | tf_op jit(solution)/shard_map/psum | solution.py:260
  108.7 4.4 %outputs.1 = (bf16[256,3072]{1,0:T(8,128)(2,1)}, bf16[256,1024]{1,0:T(8,128)(2,1)}) custom-call(bf16[1024,512]{1,0:T(8,128)(2,1)} %get-tuple-element.114.gate_far, bf16[1024,512]{1,0:T(8,128)(2,1)} %get-tuple-element.115.up_far, bf16[1024,512]{1,0:T(8,128)(2,1)} %get-tuple-element.116.down_far, bf16[64,128]{1,0:T(8,128)(2,1)S(1)} %get-tuple-element.223.refs_0_, ...), custom_call_target="tpu_custom_call" | custom-call | tf_op jit(solution)/shard_map/outputs/pallas_call | solution.py:26
  113.1 17.3 %all-to-all-start.1 = ((bf16[32,8,1024]{2,1,0:T(8,128)(2,1)}), bf16[32,8,1024]{2,1,0:T(8,128)(2,1)S(1)}, u32[]{:S(2)}, u32[]{:S(2)}) async-start(bf16[32,8,1024]{2,1,0:T(8,128)(2,1)} %bitcast.7), calls=%async_computation.1 | async-start | bytes 1048576 | tf_op jit(solution)/shard_map/all_to_all | solution.py:277
  130.4 0.0 copy-start
  130.4 1.4 copy-done
  131.8 4.0 %grads.3 = (f32[10,128,128]{2,1,0:T(8,128)}, f32[10,128,128]{2,1,0:T(8,128)}, f32[10,128,128]{2,1,0:T(8,128)}) custom-call(s32[3,10]{1,0:T(4,128)S(1)} %pad_add_fusion.slots, bf16[256,1024]{1,0:T(8,128)(2,1)S(1)} %bitcast.12, bf16[256,3072]{1,0:T(8,128)(2,1)S(1)} %copy-done), custom_call_target="tpu_custom_call" | custom-call | tf_op jit(solution)/shard_map/grads/pallas_call | solution.py:26
  135.7 6.2 %all-to-all-done.1.parts = bf16[32,8,1024]{2,1,0:T(8,128)(2,1)S(1)} async-done(((bf16[32,8,1024]{2,1,0:T(8,128)(2,1)}), bf16[32,8,1024]{2,1,0:T(8,128)(2,1)S(1)}, u32[]{:S(2)}, u32[]{:S(2)}) %all-to-all-start.1) | async-done | bytes 524320 | tf_op jit(solution)/shard_map/all_to_all | solution.py:277
  142.0 0.7 row_sum.1
  (1 shorter events, 0.0 us)
Async XLA Ops:
  0.6 28.0 %copy-start.4 = (s32[1,1,10]{2,1,0:T(1,128)S(1)}, s32[1,1,10]{2,1,0:T(1,128)}, u32[]{:S(2)}) copy-start(s32[1,1,10]{2,1,0:T(1,128)} %param.14) | copy-start | bytes 124
  0.6 28.0 %copy-start.5 = (s32[1,1,10]{2,1,0:T(1,128)S(1)}, s32[1,1,10]{2,1,0:T(1,128)}, u32[]{:S(2)}) copy-start(s32[1,1,10]{2,1,0:T(1,128)} %param.13) | copy-start | bytes 124
  0.7 28.0 %copy-start.6 = (s32[1,1,10]{2,1,0:T(1,128)S(1)}, s32[1,1,10]{2,1,0:T(1,128)}, u32[]{:S(2)}) copy-start(s32[1,1,10]{2,1,0:T(1,128)} %param.12) | copy-start | bytes 124
  0.7 28.1 %copy-start.3 = (bf16[1,1,10,128,128]{4,3,2,1,0:T(8,128)(2,1)S(1)}, bf16[1,1,10,128,128]{4,3,2,1,0:T(8,128)(2,1)}, u32[]{:S(2)}) copy-start(bf16[1,1,10,128,128]{4,3,2,1,0:T(8,128)(2,1)} %param.11) | copy-start | bytes 983044
  0.7 28.1 %copy-start.2 = (bf16[1,1,10,128,128]{4,3,2,1,0:T(8,128)(2,1)S(1)}, bf16[1,1,10,128,128]{4,3,2,1,0:T(8,128)(2,1)}, u32[]{:S(2)}) copy-start(bf16[1,1,10,128,128]{4,3,2,1,0:T(8,128)(2,1)} %param.10) | copy-start | bytes 983044
  0.7 28.1 %copy-start.1 = (bf16[1,1,10,128,128]{4,3,2,1,0:T(8,128)(2,1)S(1)}, bf16[1,1,10,128,128]{4,3,2,1,0:T(8,128)(2,1)}, u32[]{:S(2)}) copy-start(bf16[1,1,10,128,128]{4,3,2,1,0:T(8,128)(2,1)} %param.9) | copy-start | bytes 983044
  18.3 22.1 %all-to-all-start = ((bf16[32,8,1024]{2,1,0:T(8,128)(2,1)}), bf16[32,8,1024]{2,1,0:T(8,128)(2,1)S(1)}, u32[]{:S(2)}, u32[]{:S(2)}) async-start(bf16[32,8,1024]{2,1,0:T(8,128)(2,1)} %spread.1), calls=%async_computation | async-start | bytes 1048576 | tf_op jit(solution)/shard_map/all_to_all | solution.py:241
  113.1 28.9 %all-to-all-start.1 = ((bf16[32,8,1024]{2,1,0:T(8,128)(2,1)}), bf16[32,8,1024]{2,1,0:T(8,128)(2,1)S(1)}, u32[]{:S(2)}, u32[]{:S(2)}) async-start(bf16[32,8,1024]{2,1,0:T(8,128)(2,1)} %bitcast.7), calls=%async_computation.1 | async-start | bytes 1048576 | tf_op jit(solution)/shard_map/all_to_all | solution.py:277
  130.4 1.4 copy-start

commit v7 on v4

--- a/solution.py
+++ b/solution.py
@@ -49,21 +49,31 @@
     )
 
 
-def spread_kernel(tokens, grads, out):
+def spread_kernel(tokens, grads, out, near, sems):
     width = tokens.shape[1]
-    out[:, :, :width] = jnp.broadcast_to(tokens[...][None], (out.shape[0],) + tokens.shape)
-    out[:, :, width:] = jnp.broadcast_to(grads[...][None], (out.shape[0],) + grads.shape)
+    copies = [
+        pltpu.make_async_copy(tokens, near.at[0], sems.at[0]),
+        pltpu.make_async_copy(grads, near.at[1], sems.at[1]),
+    ]
+    for copy in copies:
+        copy.start()
+    for half, copy in enumerate(copies):
+        copy.wait()
+        out[:, :, half * width : (half + 1) * width] = jnp.broadcast_to(
+            near[half][None], (out.shape[0],) + tokens.shape
+        )
 
 
 def place_kernel(
-    slots, gate_blk, up_blk, down_blk, gate_ref, up_out, down_out, up_ref, down_ref, sems
+    slots, gate_blk, up_blk, down_blk, gate_out, up_out, down_out, gate_ref, up_ref, down_ref, sems
 ):
-    tiles = ((down_blk, down_ref, 2), (up_blk, up_ref, 1), (gate_blk, gate_ref, 0))
-    copies = {
-        1: pltpu.make_async_copy(up_ref, up_out, sems.at[0]),
-        2: pltpu.make_async_copy(down_ref, down_out, sems.at[1]),
-    }
-    for blk, ref, which in tiles:
+    tiles = (
+        (gate_blk, gate_ref, gate_out),
+        (up_blk, up_ref, up_out),
+        (down_blk, down_ref, down_out),
+    )
+    copies = []
+    for which, (blk, ref, out) in enumerate(tiles):
         ref[...] = jnp.zeros_like(ref)
         col_blocks = ref.shape[1] // BLK
         total = (ref.shape[0] // BLK) * col_blocks
@@ -74,35 +84,37 @@
             def _(number=number, slot=slot, blk=blk, ref=ref, col_blocks=col_blocks):
                 ref[at(number // col_blocks, BLK), at(number % col_blocks, BLK)] = blk[slot]
 
-        if which > 0:
-            copies[which].start()
-    copies[1].wait()
-    copies[2].wait()
-
-
-def partial_kernel(panel, gate_w, up_far, down_far, *refs):
-    outs, (up_w, down_w, sems) = refs[:-3], refs[-3:]
-    copies = {
-        1: pltpu.make_async_copy(up_far, up_w, sems.at[0]),
-        2: pltpu.make_async_copy(down_far, down_w, sems.at[1]),
-    }
-    copies[1].start()
-    copies[2].start()
+        copies.append(pltpu.make_async_copy(ref, out, sems.at[which]))
+        copies[-1].start()
+    for copy in copies:
+        copy.wait()
+
+
+def partial_kernel(panel, gate_far, up_far, down_far, panel_out, *refs):
+    outs, (gate_w, up_w, down_w, sems) = refs[:-4], refs[-4:]
+    pairs = ((gate_far, gate_w), (up_far, up_w), (down_far, down_w))
+    loads = [pltpu.make_async_copy(far, near, sems.at[i]) for i, (far, near) in enumerate(pairs)]
+    for load in loads:
+        load.start()
+    keep = pltpu.make_async_copy(panel, panel_out, sems.at[3])
+    keep.start()
     width, hid = gate_w.shape
     blocks = hid // BLK
     jobs = ((0, gate_w, 0), (0, up_w, 0), (width, down_w, 1))
     each = len(outs) // 3
     for which, (lo, weight, dim) in enumerate(jobs):
-        if which > 0:
-            copies[which].wait()
+        loads[which].wait()
         term = dot(panel[:, lo : lo + width], weight[...], 1, dim).astype(BF16)
         for i in range(each):
             row, col = (i // blocks) * GROUP, (i % blocks) * BLK
             outs[which * each + i][...] = term[row : row + GROUP, col : col + BLK]
-
-
-def output_kernel(gate_w, up_far, down_far, *refs):
-    sums, (panel_out, out, panel, up_w, down_w, sems) = refs[:-6], refs[-6:]
+    keep.wait()
+
+
+def output_kernel(gate_far, up_far, down_far, *refs):
+    sums, (panel_out, out, panel, gate_w, up_w, down_w, sems) = refs[:-7], refs[-7:]
+    load_gate = pltpu.make_async_copy(gate_far, gate_w, sems.at[3])
+    load_gate.start()
     load_up = pltpu.make_async_copy(up_far, up_w, sems.at[0])
     load = pltpu.make_async_copy(down_far, down_w, sems.at[1])
     store = pltpu.make_async_copy(panel, panel_out, sems.at[2])
@@ -123,6 +135,7 @@
         ).astype(BF16)
         panel[rows, 2 * hid + col : 2 * hid + col + BLK] = (cot * act).astype(BF16)
     store.start()
+    load_gate.wait()
     load_up.wait()
     out[:, width:] = (
         dot(panel[:, hid : 2 * hid], gate_w[...], 1, 1)
@@ -184,29 +197,39 @@
         (((width, hid), BF16), ((width, hid), BF16), ((hid, width), BF16)),
         (
             pltpu.VMEM((width, hid), BF16),
+            pltpu.VMEM((width, hid), BF16),
             pltpu.VMEM((hid, width), BF16),
-            pltpu.SemaphoreType.DMA((2,)),
+            pltpu.SemaphoreType.DMA((3,)),
         ),
         name="place",
-        far_outs=(1, 2),
+        far_outs=(0, 1, 2),
     )
     (spread,) = call(
-        spread_kernel, (), (tokens, out_grad), (((n_row, local, 2 * width), BF16),), name="spread"
+        spread_kernel,
+        (),
+        (tokens, out_grad),
+        (((n_row, local, 2 * width), BF16),),
+        (pltpu.VMEM((2, local, width), BF16), pltpu.SemaphoreType.DMA((2,))),
+        name="spread",
+        far=(0, 1),
     )
     panel = lax.all_to_all(spread, "row", 0, 0, tiled=True).reshape(count, 2 * width)
 
-    terms = call(
+    n_blocks = 3 * (count // GROUP) * (hid // BLK)
+    kept, *terms = call(
         partial_kernel,
         (),
         (panel, gate_w, up_w, down_w),
-        (((GROUP, BLK), BF16),) * (3 * (count // GROUP) * (hid // BLK)),
-        (
+        (((count, 2 * width), BF16),) + (((GROUP, BLK), BF16),) * n_blocks,
+        (
+            pltpu.VMEM((width, hid), BF16),
             pltpu.VMEM((width, hid), BF16),
             pltpu.VMEM((hid, width), BF16),
-            pltpu.SemaphoreType.DMA((2,)),
+            pltpu.SemaphoreType.DMA((4,)),
         ),
         name="partials",
-        far=(2, 3),
+        far=(1, 2, 3),
+        far_outs=(0,),
     )
     sums = lax.psum(tuple(terms), "col")
     hidden, out_terms = call(
@@ -217,11 +240,12 @@
         (
             pltpu.VMEM((count, wide), BF16),
             pltpu.VMEM((width, hid), BF16),
+            pltpu.VMEM((width, hid), BF16),
             pltpu.VMEM((hid, width), BF16),
-            pltpu.SemaphoreType.DMA((3,)),
+            pltpu.SemaphoreType.DMA((4,)),
         ),
         name="outputs",
-        far=(1, 2),
+        far=(0, 1, 2),
         far_outs=(0,),
     )
     parts = lax.all_to_all(
@@ -230,7 +254,7 @@
     gate_grad, up_grad, down_grad = call(
         grad_kernel,
         (slots,),
-        (panel, hidden),
+        (kept, hidden),
         tuple((ref.shape[2:], F32) for ref in (gate_blocks, up_blocks, down_blocks)),
         (
             pltpu.VMEM((width // BLK, BLK, count), BF16),

time: 163 us -> 126 us (0.77)
  local copies, waits for them, and re-layouts: 39.9 us -> 1.43 us
  Pallas kernels: 14.2 us -> 16.6 us
    unnamed x162 -> x16, local copies, waits for them, and re-layouts: 39.9 us -> 1.43 us
    pallas_call x6, Pallas kernels: 14.2 us -> 16.6 us  [call(): pl.pallas_call(kernel, out_shape=[pltpu.HBM(*out) if i in far_outs else j...]
  transfers between devices with their start and end apart: 2 -> 2, of which waited for: 2 -> 2; matrix products, arithmetic and copies ran while one was open for 0% -> 0% of each run, Pallas kernels for 4% -> 6%
where the time goes in v7:
time: 126 us; the launch traced here: 125 us
  blocking collectives  64.1 us (51%)
  starting transfers between devices  27.8 us (22%)
  Pallas kernels  16.6 us (13%)
  waiting for transfers between devices  14.3 us (11%)
  local copies, waits for them, and re-layouts  1.43 us (1%)
    psum x1, blocking collectives, per_device(): sums = lax.psum(tuple(terms), 'col')  64.1 us
    all_to_all x1, starting transfers between devices, per_device(): lax.all_to_all(out_terms.reshape(n_row, local, 2 * width), 'row', 0, 0, t...  17.4 us
    pallas_call x6, Pallas kernels, call(): pl.pallas_call(kernel, out_shape=[pltpu.HBM(*out) if i in far_outs else j...  16.6 us
    all_to_all x1, starting transfers between devices, per_device(): lax.all_to_all(spread, 'row', 0, 0, tiled=True).reshape(count, 2 * width)  10.4 us
    all_to_all x1, waiting for transfers between devices, per_device(): lax.all_to_all(spread, 'row', 0, 0, tiled=True).reshape(count, 2 * width)  9.18 us
    all_to_all x1, waiting for transfers between devices, per_device(): lax.all_to_all(out_terms.reshape(n_row, local, 2 * width), 'row', 0, 0, t...  5.12 us
  transfers between devices with their start and end apart: 2, of which 2 were waited for; matrix products, arithmetic and copies ran while one was open for 0% of the time, Pallas kernels for 6%

profile of v7, /device:TPU:1, one launch (start us, length us, event | category | flops | bytes accessed | tf_op | source)
XLA Modules:
  0.0 125.1 jit_solution(13282851903968934236)
XLA Ops:
  0.6 0.0 copy-start.5
  0.6 0.0 copy-start.6
  0.7 0.0 copy-start.7
  0.7 0.0 copy-start.4
  0.7 0.0 copy-start.3
  0.7 0.0 copy-start.2
  0.7 1.7 %spread.1 = bf16[32,8,1024]{2,1,0:T(8,128)(2,1)} custom-call(bf16[8,512]{1,0:T(8,128)(2,1)} %tokens.1, bf16[8,512]{1,0:T(8,128)(2,1)} %grads.2), custom_call_target="tpu_custom_call" | custom-call | tf_op jit(solution)/shard_map/spread/pallas_call | solution.py:25
  2.4 10.4 %all-to-all-start = ((bf16[32,8,1024]{2,1,0:T(8,128)(2,1)}), bf16[32,8,1024]{2,1,0:T(8,128)(2,1)S(1)}, u32[]{:S(2)}, u32[]{:S(2)}) async-start(bf16[32,8,1024]{2,1,0:T(8,128)(2,1)} %spread.1), calls=%async_computation | async-start | bytes 1048576 | tf_op jit(solution)/shard_map/all_to_all | solution.py:216
  12.8 0.0 copy-done.5
  12.8 0.0 copy-done.6
  12.8 0.0 copy-done.7
  12.8 0.0 copy-done.4
  12.8 0.0 copy-done.3
  12.8 0.0 copy-done.2
  12.8 2.4 %place.1 = (bf16[512,1024]{1,0:T(8,128)(2,1)}, bf16[512,1024]{1,0:T(8,128)(2,1)}, bf16[1024,512]{1,0:T(8,128)(2,1)}) custom-call(s32[3,10]{1,0:T(4,128)S(1)} %pad_add_fusion.slots, bf16[10,128,128]{2,1,0:T(8,128)(2,1)S(1)} %bitcast.12, bf16[10,128,128]{2,1,0:T(8,128)(2,1)S(1)} %bitcast.13, bf16[10,128,128]{2,1,0:T(8,128)(2,1)S(1)} %bitcast.14), custom_call_target="tpu_custom_call" | custom-call | tf_op jit(solution)/shard_map/place/pallas_call | solution.py:25
  15.3 9.2 %all-to-all-done = bf16[32,8,1024]{2,1,0:T(8,128)(2,1)S(1)} async-done(((bf16[32,8,1024]{2,1,0:T(8,128)(2,1)}), bf16[32,8,1024]{2,1,0:T(8,128)(2,1)S(1)}, u32[]{:S(2)}, u32[]{:S(2)}) %all-to-all-start) | async-done | bytes 524320 | tf_op jit(solution)/shard_map/all_to_all | solution.py:216
  24.5 2.8 %partials.1 = (bf16[256,1024]{1,0:T(8,128)(2,1)}, bf16[64,128]{1,0:T(8,128)(2,1)S(1)}, bf16[64,128]{1,0:T(8,128)(2,1)S(1)}, bf16[64,128]{1,0:T(8,128)(2,1)S(1)},...) custom-call(bf16[256,1024]{1,0:T(8,128)(2,1)S(1)} %bitcast.11, ...), custom_call_target="tpu_custom_call" | custom-call | tf_op jit(solution)/shard_map/partials/pallas_call | solution.py:25
  27.3 64.1 %all-reduce.2 = (bf16[64,128]{1,0:T(8,128)(2,1)S(1)}, bf16[64,128]{1,0:T(8,128)(2,1)S(1)}, bf16[64,128]{1,0:T(8,128)(2,1)S(1)}, bf16[64,128]{1,0:T(8,128)(2,1)S(...) all-reduce(bf16[64,128]{1,0:T(8,128)(2,1)S(1)} %get-tuple-element.1, ...), channel_id=1, replica_groups=mesh['row'=32,'col'=16] {'col'}, use_global_device_ids=true, to_apply=%region_0.0 | all-reduce | flops 786432 | bytes 3145728 | tf_op jit(solution)/shard_map/psum | solution.py:234
  91.4 0.0 copy-start.1
  91.4 3.9 %outputs.1 = (bf16[256,3072]{1,0:T(8,128)(2,1)}, bf16[256,1024]{1,0:T(8,128)(2,1)}) custom-call(bf16[512,1024]{1,0:T(8,128)(2,1)} %get-tuple-element.112.gate_far, bf16[512,1024]{1,0:T(8,128)(2,1)} %get-tuple-element.113.up_far, bf16[1024,512]{1,0:T(8,128)(2,1)} %get-tuple-element.114.down_far, bf16[64,128]{1,0:T(8,128)(2,1)S(1)} %get-tuple-element.219.refs_0_, ...), custom_call_target="tpu_custom_call" | custom-call | tf_op jit(solution)/shard_map/outputs/pallas_call | solution.py:25
  95.3 17.4 %all-to-all-start.1 = ((bf16[32,8,1024]{2,1,0:T(8,128)(2,1)}), bf16[32,8,1024]{2,1,0:T(8,128)(2,1)S(1)}, u32[]{:S(2)}, u32[]{:S(2)}) async-start(bf16[32,8,1024]{2,1,0:T(8,128)(2,1)} %bitcast.7), calls=%async_computation.1 | async-start | bytes 1048576 | tf_op jit(solution)/shard_map/all_to_all | solution.py:251
  112.7 0.0 copy-done.1
  112.7 0.0 copy-start
  112.7 1.4 %copy-done = bf16[256,3072]{1,0:T(8,128)(2,1)S(1)} copy-done((bf16[256,3072]{1,0:T(8,128)(2,1)S(1)}, bf16[256,3072]{1,0:T(8,128)(2,1)}, u32[]{:S(2)}) %copy-start) | copy-done | bytes 1572888
  114.1 5.1 %grads.3 = (f32[10,128,128]{2,1,0:T(8,128)}, f32[10,128,128]{2,1,0:T(8,128)}, f32[10,128,128]{2,1,0:T(8,128)}) custom-call(s32[3,10]{1,0:T(4,128)S(1)} %pad_add_fusion.slots, bf16[256,1024]{1,0:T(8,128)(2,1)S(1)} %copy-done.1, bf16[256,3072]{1,0:T(8,128)(2,1)S(1)} %copy-done), custom_call_target="tpu_custom_call" | custom-call | tf_op jit(solution)/shard_map/grads/pallas_call | solution.py:25
  119.3 5.1 %all-to-all-done.1.parts = bf16[32,8,1024]{2,1,0:T(8,128)(2,1)S(1)} async-done(((bf16[32,8,1024]{2,1,0:T(8,128)(2,1)}), bf16[32,8,1024]{2,1,0:T(8,128)(2,1)S(1)}, u32[]{:S(2)}, u32[]{:S(2)}) %all-to-all-start.1) | async-done | bytes 524320 | tf_op jit(solution)/shard_map/all_to_all | solution.py:251
  124.4 0.7 row_sum.1
  (1 shorter events, 0.0 us)
Async XLA Ops:
  0.6 12.1 %copy-start.5 = (s32[1,1,10]{2,1,0:T(1,128)S(1)}, s32[1,1,10]{2,1,0:T(1,128)}, u32[]{:S(2)}) copy-start(s32[1,1,10]{2,1,0:T(1,128)} %param.14) | copy-start | bytes 124
  0.6 12.1 %copy-start.6 = (s32[1,1,10]{2,1,0:T(1,128)S(1)}, s32[1,1,10]{2,1,0:T(1,128)}, u32[]{:S(2)}) copy-start(s32[1,1,10]{2,1,0:T(1,128)} %param.13) | copy-start | bytes 124
  0.7 12.1 %copy-start.7 = (s32[1,1,10]{2,1,0:T(1,128)S(1)}, s32[1,1,10]{2,1,0:T(1,128)}, u32[]{:S(2)}) copy-start(s32[1,1,10]{2,1,0:T(1,128)} %param.12) | copy-start | bytes 124
  0.7 12.1 %copy-start.4 = (bf16[1,1,10,128,128]{4,3,2,1,0:T(8,128)(2,1)S(1)}, bf16[1,1,10,128,128]{4,3,2,1,0:T(8,128)(2,1)}, u32[]{:S(2)}) copy-start(bf16[1,1,10,128,128]{4,3,2,1,0:T(8,128)(2,1)} %param.11) | copy-start | bytes 983044
  0.7 12.1 %copy-start.3 = (bf16[1,1,10,128,128]{4,3,2,1,0:T(8,128)(2,1)S(1)}, bf16[1,1,10,128,128]{4,3,2,1,0:T(8,128)(2,1)}, u32[]{:S(2)}) copy-start(bf16[1,1,10,128,128]{4,3,2,1,0:T(8,128)(2,1)} %param.10) | copy-start | bytes 983044
  0.7 12.1 %copy-start.2 = (bf16[1,1,10,128,128]{4,3,2,1,0:T(8,128)(2,1)S(1)}, bf16[1,1,10,128,128]{4,3,2,1,0:T(8,128)(2,1)}, u32[]{:S(2)}) copy-start(bf16[1,1,10,128,128]{4,3,2,1,0:T(8,128)(2,1)} %param.9) | copy-start | bytes 983044
  2.4 22.1 %all-to-all-start = ((bf16[32,8,1024]{2,1,0:T(8,128)(2,1)}), bf16[32,8,1024]{2,1,0:T(8,128)(2,1)S(1)}, u32[]{:S(2)}, u32[]{:S(2)}) async-start(bf16[32,8,1024]{2,1,0:T(8,128)(2,1)} %spread.1), calls=%async_computation | async-start | bytes 1048576 | tf_op jit(solution)/shard_map/all_to_all | solution.py:216
  91.4 21.3 %copy-start.1 = (bf16[256,1024]{1,0:T(8,128)(2,1)S(1)}, bf16[256,1024]{1,0:T(8,128)(2,1)}, u32[]{:S(2)}) copy-start(bf16[256,1024]{1,0:T(8,128)(2,1)} %get-tuple-element.214.panel) | copy-start | bytes 1572868
  95.3 29.1 %all-to-all-start.1 = ((bf16[32,8,1024]{2,1,0:T(8,128)(2,1)}), bf16[32,8,1024]{2,1,0:T(8,128)(2,1)S(1)}, u32[]{:S(2)}, u32[]{:S(2)}) async-start(bf16[32,8,1024]{2,1,0:T(8,128)(2,1)} %bitcast.7), calls=%async_computation.1 | async-start | bytes 1048576 | tf_op jit(solution)/shard_map/all_to_all | solution.py:251
  112.7 1.4 %copy-start = (bf16[256,3072]{1,0:T(8,128)(2,1)S(1)}, bf16[256,3072]{1,0:T(8,128)(2,1)}, u32[]{:S(2)}) copy-start(bf16[256,3072]{1,0:T(8,128)(2,1)} %get-tuple-element.215.hidden) | copy-start | bytes 4718596
